TPU v7x, 256 devices: a whole 4x4x8 slice. The times are simulated.
256 devices in a mesh: tm: 8 (over z_hi, y), space: 32 (over z_lo, x, core).
Axes of the slice: x: 4, y: 4, z: 8 (z_hi: 2, z_lo: 4; z = z_hi * 4 + z_lo), core: 2. Of those that a mesh axis runs over, the one named last changes fastest.
Arguments:
- member_average: float32 [128, 2880, 640], P('tm', 'space'), may hold values from -6 to 6
- member_spread_squared: float32 [128, 2880, 640], P('tm', 'space'), may hold values from 0.1 to 4
- measured_truth: float32 [128, 2880, 640], P('tm', 'space'), may hold values from -8 to 8
- coefficients: float32 [4, 2880, 640], P(None, 'space'), may hold values from -1 to 1
Outputs:
- updated: float32 [4, 2880, 640], P(None, 'space')
All inputs are finite; a program needn't handle non-finite values.
Results may differ from a plain program's by a relative error of at most 0.00002.
Values sent between devices are 32-bit elements; how exact they have to be, the bound alone decides.
No kernel may reach another device: no remote copies, remote signals or barrier semaphores. Data moves between devices by JAX's collectives and lax.ppermute only.
A program may use at most 64 MiB of HBM per device.

v0:
```python
import jax
import jax.numpy as jnp
from jax import lax
from jax.sharding import PartitionSpec as P

ITERS = 2


descent_factor = 0.5
smooth_weight = 0.03


def padded(block, sides, width):
    for axis, dim in sides:
        count = lax.axis_size(axis)
        forward = [(i, i + 1) for i in range(count - 1)]
        forward.append((count - 1, 0))
        backward = [(target, source) for source, target in forward]
        low = lax.ppermute(
            lax.slice_in_dim(block, block.shape[dim] - width, None, axis=dim), axis, forward
        )
        high = lax.ppermute(lax.slice_in_dim(block, 0, width, axis=dim), axis, backward)
        block = jnp.concatenate([low, block, high], axis=dim)
    return block


def laplace_rim(extended):
    middle = extended[:, 1:-1, :]
    along_lon = extended[:, 2:, :] + extended[:, :-2, :] - 2.0 * middle
    steps_lat = middle[..., 1:] - middle[..., :-1]
    zero_col = jnp.zeros(middle.shape[:-1] + (1,), jnp.float32)
    along_lat = jnp.concatenate([steps_lat, zero_col], axis=-1) - jnp.concatenate(
        [zero_col, steps_lat], axis=-1
    )
    return along_lon + along_lat


def daily_score_parts(calibration_coefficients_set, fmean, fvar, obs):
    base_exp = jnp.exp(calibration_coefficients_set[2])
    spread = jnp.sqrt(
        base_exp + calibration_coefficients_set[3] * calibration_coefficients_set[3] * fvar
    )
    center = calibration_coefficients_set[0] + calibration_coefficients_set[1] * fmean
    standard = (obs - center) / spread
    cumulative = 0.5 * (1.0 + jax.scipy.special.erf(standard * 0.7071067811865476))
    density = jnp.exp(-0.5 * standard * standard) * 0.3989422804014327
    dcenter = 1.0 - 2.0 * cumulative
    dvar = (2.0 * density - 0.5641895835477563) / (2.0 * spread)
    return jnp.stack(
        [
            jnp.sum(dcenter, axis=0),
            jnp.sum(dcenter * fmean, axis=0),
            jnp.sum(dvar * base_exp, axis=0),
            jnp.sum(dvar * 2.0 * calibration_coefficients_set[3] * fvar, axis=0),
        ]
    )


def smoothing(calibration_coefficients_set):
    first = laplace_rim(padded(calibration_coefficients_set, (("space", 1),), 1))
    return laplace_rim(padded(first, (("space", 1),), 1))


def apply_update(calibration_coefficients_set, partial_sum, roughness_cost, every_day_total):
    aggregate_loss = lax.psum(partial_sum, "tm")
    return calibration_coefficients_set - descent_factor * (
        aggregate_loss / every_day_total + roughness_cost
    )


def on_device(member_average, member_spread_squared, measured_truth, coefficients):
    calibration_coefficients_set = coefficients
    every_day_total = member_average.shape[0] * lax.axis_size("tm")
    for step in range(ITERS):
        partial_sum = daily_score_parts(
            calibration_coefficients_set, member_average, member_spread_squared, measured_truth
        )
        roughness_cost = smooth_weight * smoothing(calibration_coefficients_set)
        calibration_coefficients_set = apply_update(
            calibration_coefficients_set, partial_sum, roughness_cost, every_day_total
        )
    return calibration_coefficients_set


def solution(mesh):
    placed = (
        P("tm", "space", None),
        P("tm", "space", None),
        P("tm", "space", None),
        P(None, "space", None),
    )
    return jax.shard_map(
        on_device, mesh=mesh, in_specs=placed, out_specs=P(None, "space", None), check_vma=False
    )
```

profile of v0, /device:TPU:64, one launch (start us, length us, event | category | flops | bytes accessed | tf_op | source)
XLA Modules:
  0.0 267.8 jit_solution(1380413186751168871)
XLA Ops:
  6.5 0.0 all-reduce.11.cloned.1.call-start
  6.5 0.0 copy-start
  6.5 1.4 copy.16
  7.9 0.1 multiply_bitcast_fusion.2
  8.0 0.8 copy-done
  8.9 5.4 %add_subtract_fusion.1 = (f32[16,90,640]{2,0,1:T(8,128)S(1)}, f32[16,90,640]{2,0,1:T(8,128)S(1)}) fusion(f32[16,90,640]{2,0,1:T(8,128)} %param.5, f32[90,640]{1,0:T(8,128)S(1)} %get-tuple-element.27, f32[90,640]{1,0:T(8,128)S(1)} %get-tuple-element.28, f32[16,90,640]{2,0,1:T(8,128)} %param.6, f32[16,90,640]{2,0,1:T(8,128)S(1)} %copy-done, ...), kind=kLoop, calls=%fused_computation.19 | loop fusion | flops 8294400 | bytes 19353600 | tf_op jit(solution)/shard_map/sub | solution.py:47
  14.3 0.0 copy-start.2
  14.3 1.7 fusion.31
  15.9 0.4 copy-done.2
  16.3 4.6 %multiply_reduce_fusion.4 = (f32[90,640]{1,0:T(8,128)S(1)}, f32[90,640]{1,0:T(8,128)S(1)}) fusion(f32[90,640]{1,0:T(8,128)S(1)} %get-tuple-element.28, f32[16,90,640]{2,0,1:T(8,128)S(1)} %copy-done.2, f32[90,640]{1,0:T(8,128)S(1)} %get-tuple-element.27, f32[16,90,640]{2,0,1:T(8,128)S(1)} %get-tuple-element.16, f32[90,640]{1,0:T(8,128)S(1)} %get-tuple-element.26), kind=kLoop, calls=%fused_computation.17 | loop fusion | flops 11865600 | bytes 8524800 | tf_op jit(solution)/shard_map/reduce_sum | solution.py:53
  20.9 1.0 pad_maximum_fusion.8
  22.0 0.0 all-reduce.11.cloned.1.call-update
  22.0 0.0 all-reduce.13.cloned.1.call-start
  22.0 0.7 fusion.35
  22.8 1.8 collective-permute-start
  24.6 0.1 collective-permute-start.1
  24.7 0.3 slice_subtract_fusion.3
  25.0 1.0 collective-permute-done
  26.0 3.9 %collective-permute-done.1 = f32[4,1,640]{2,1,0:T(1,128)S(1)} collective-permute-done((f32[4,1,640]{2,1,0:T(1,128)S(1)}, f32[4,1,640]{2,1,0:T(1,128)S(1)}, u32[]{:S(2)}, u32[]{:S(2)}) %collective-permute-start.1) | collective-permute-done | bytes 10272 | tf_op jit(solution)/shard_map/ppermute | solution.py:19
  29.9 0.4 fusion.27
  30.3 0.1 collective-permute-start.2
  30.4 0.5 collective-permute-start.3
  30.9 0.3 slice_subtract_fusion.2
  31.3 0.6 collective-permute-done.2
  31.8 4.1 %collective-permute-done.3 = f32[4,1,640]{2,1,0:T(1,128)S(1)} collective-permute-done((f32[4,1,640]{2,1,0:T(1,128)S(1)}, f32[4,1,640]{2,1,0:T(1,128)S(1)}, u32[]{:S(2)}, u32[]{:S(2)}) %collective-permute-start.3) | collective-permute-done | bytes 10272 | tf_op jit(solution)/shard_map/ppermute | solution.py:19
  35.9 98.4 %all-reduce.11.cloned.1.call-done = f32[4,90,640]{2,1,0:T(8,128)} async-done(((f32[4,90,640]{2,1,0:T(8,128)}), f32[4,90,640]{2,1,0:T(8,128)}) %all-reduce.11.cloned.1.call-update) | async-done | bytes 921616 | tf_op jit(solution)/shard_map/psum | solution.py:65
  134.3 0.0 copy-start.1
  134.3 2.2 fusion.24
  136.5 0.1 multiply_bitcast_fusion
  136.6 0.3 copy-done.1
  136.9 5.4 %add_subtract_fusion = (f32[16,90,640]{2,0,1:T(8,128)S(1)}, f32[16,90,640]{2,0,1:T(8,128)S(1)}) fusion(f32[16,90,640]{2,0,1:T(8,128)} %param.5, f32[90,640]{1,0:T(8,128)S(1)} %get-tuple-element.18, f32[90,640]{1,0:T(8,128)S(1)} %get-tuple-element.19, f32[16,90,640]{2,0,1:T(8,128)} %param.6, f32[16,90,640]{2,0,1:T(8,128)S(1)} %copy-done.1, ...), kind=kLoop, calls=%fused_computation.13 | loop fusion | flops 8294400 | bytes 19353600 | tf_op jit(solution)/shard_map/sub | solution.py:47
  142.3 0.0 copy-start.3
  142.3 1.7 fusion.30
  144.0 0.4 copy-done.3
  144.3 4.6 %multiply_reduce_fusion.1 = (f32[90,640]{1,0:T(8,128)S(1)}, f32[90,640]{1,0:T(8,128)S(1)}) fusion(f32[90,640]{1,0:T(8,128)S(1)} %get-tuple-element.19, f32[16,90,640]{2,0,1:T(8,128)S(1)} %copy-done.3, f32[90,640]{1,0:T(8,128)S(1)} %get-tuple-element.18, f32[16,90,640]{2,0,1:T(8,128)S(1)} %get-tuple-element.14, f32[90,640]{1,0:T(8,128)S(1)} %get-tuple-element.17), kind=kLoop, calls=%fused_computation.11 | loop fusion | flops 11865600 | bytes 8524800 | tf_op jit(solution)/shard_map/reduce_sum | solution.py:53
  149.0 1.0 pad_maximum_fusion.9
  150.0 0.0 all-reduce.13.cloned.1.call-update
  150.0 0.1 collective-permute-start.4
  150.1 0.5 collective-permute-start.5
  150.6 0.3 slice_subtract_fusion.1
  150.9 0.6 collective-permute-done.4
  151.5 3.9 %collective-permute-done.5 = f32[4,1,640]{2,1,0:T(1,128)S(1)} collective-permute-done((f32[4,1,640]{2,1,0:T(1,128)S(1)}, f32[4,1,640]{2,1,0:T(1,128)S(1)}, u32[]{:S(2)}, u32[]{:S(2)}) %collective-permute-start.5) | collective-permute-done | bytes 10272 | tf_op jit(solution)/shard_map/ppermute | solution.py:19
  155.4 0.4 fusion.17
  155.9 0.1 collective-permute-start.6
  155.9 0.5 collective-permute-start.7
  156.4 0.3 slice_subtract_fusion
  156.8 0.6 collective-permute-done.6
  157.3 3.9 %collective-permute-done.7 = f32[4,1,640]{2,1,0:T(1,128)S(1)} collective-permute-done((f32[4,1,640]{2,1,0:T(1,128)S(1)}, f32[4,1,640]{2,1,0:T(1,128)S(1)}, u32[]{:S(2)}, u32[]{:S(2)}) %collective-permute-start.7) | collective-permute-done | bytes 10272 | tf_op jit(solution)/shard_map/ppermute | solution.py:19
  161.2 96.4 %all-reduce.13.cloned.1.call-done = f32[4,90,640]{2,1,0:T(8,128)} async-done(((f32[4,90,640]{2,1,0:T(8,128)}), f32[4,90,640]{2,1,0:T(8,128)}) %all-reduce.13.cloned.1.call-update) | async-done | bytes 921616 | tf_op jit(solution)/shard_map/psum | solution.py:65
  257.6 1.8 fusion.14
  259.4 1.5 copy.17
  (5 shorter events, 0.1 us)
Async XLA Ops:
  6.5 127.7 %all-reduce.11.cloned.1.call-start = ((), (), s32[]{:S(2)}) async-start(), calls=%async_computation | async-start | bytes 1966080 | tf_op jit(solution)/shard_map/psum | solution.py:65
  6.5 2.3 copy-start
  14.3 2.0 copy-start.2
  22.0 235.6 %all-reduce.13.cloned.1.call-start = ((), (), s32[]{:S(2)}) async-start(), calls=%async_computation.1 | async-start | bytes 1966080 | tf_op jit(solution)/shard_map/psum | solution.py:65
  22.8 3.2 %collective-permute-start = (f32[4,1,640]{2,1,0:T(1,128)S(1)}, f32[4,1,640]{2,1,0:T(1,128)S(1)}, u32[]{:S(2)}, u32[]{:S(2)}) collective-permute-start(f32[4,1,640]{2,1,0:T(1,128)S(1)} %copy.9), channel_id=1, source_target_pairs={{1,0},{2,1},{3,2},{4,3},{5,4},{6,5},{7,6},{8,7},{9,8},{10,9},{11,1... | collective-permute-start | bytes 30728 | tf_op jit(solution)/shard_map/ppermute | solution.py:22
  24.6 5.3 %collective-permute-start.1 = (f32[4,1,640]{2,1,0:T(1,128)S(1)}, f32[4,1,640]{2,1,0:T(1,128)S(1)}, u32[]{:S(2)}, u32[]{:S(2)}) collective-permute-start(f32[4,1,640]{2,1,0:T(1,128)S(1)} %copy.11), channel_id=1, source_target_pairs={{0,1},{1,2},{2,3},{3,4},{4,5},{5,6},{6,7},{7,8},{8,9},{9,10},{10,1... | collective-permute-start | bytes 30728 | tf_op jit(solution)/shard_map/ppermute | solution.py:19
  30.3 1.5 collective-permute-start.2
  30.4 5.5 %collective-permute-start.3 = (f32[4,1,640]{2,1,0:T(1,128)S(1)}, f32[4,1,640]{2,1,0:T(1,128)S(1)}, u32[]{:S(2)}, u32[]{:S(2)}) collective-permute-start(f32[4,1,640]{2,1,0:T(1,128)S(1)} %get-tuple-element.32), channel_id=1, source_target_pairs={{0,1},{1,2},{2,3},{3,4},{4,5},{5,6},{6,7},{7,8},{8,9},{9,10},{10,1... | collective-permute-start | bytes 30728 | tf_op jit(solution)/shard_map/ppermute | solution.py:19
  134.3 2.6 copy-start.1
  142.3 2.0 copy-start.3
  150.0 1.5 collective-permute-start.4
  150.1 5.3 %collective-permute-start.5 = (f32[4,1,640]{2,1,0:T(1,128)S(1)}, f32[4,1,640]{2,1,0:T(1,128)S(1)}, u32[]{:S(2)}, u32[]{:S(2)}) collective-permute-start(f32[4,1,640]{2,1,0:T(1,128)S(1)} %get-tuple-element.25), channel_id=1, source_target_pairs={{0,1},{1,2},{2,3},{3,4},{4,5},{5,6},{6,7},{7,8},{8,9},{9,10},{10,1... | collective-permute-start | bytes 30728 | tf_op jit(solution)/shard_map/ppermute | solution.py:19
  155.9 1.5 collective-permute-start.6
  155.9 5.3 %collective-permute-start.7 = (f32[4,1,640]{2,1,0:T(1,128)S(1)}, f32[4,1,640]{2,1,0:T(1,128)S(1)}, u32[]{:S(2)}, u32[]{:S(2)}) collective-permute-start(f32[4,1,640]{2,1,0:T(1,128)S(1)} %get-tuple-element.23), channel_id=1, source_target_pairs={{0,1},{1,2},{2,3},{3,4},{4,5},{5,6},{6,7},{7,8},{8,9},{9,10},{10,1... | collective-permute-start | bytes 30728 | tf_op jit(solution)/shard_map/ppermute | solution.py:19
Sparse Core Ops, SparseCore 0:
  22.1 112.1 all-reduce.10
  150.1 107.4 all-reduce.12
where the time goes:
time: 271 us; the launch traced here: 268 us
  waiting for transfers between devices  213 us (79%)
  other arithmetic  31.7 us (12%)
  between operations  13.6 us (5%)
  local copies, waits for them, and re-layouts  5.58 us (2%)
  starting transfers between devices  3.69 us (1%)
    psum x2, waiting for transfers between devices, apply_update(): aggregate_loss = lax.psum(partial_sum, 'tm')  195 us
    ppermute x4, waiting for transfers between devices, padded(): lax.ppermute(lax.slice_in_dim(block, block.shape[dim] - width, None, axis...  15.8 us
    sub x2, other arithmetic, daily_score_parts(): dcenter = 1.0 - 2.0 * cumulative  10.8 us
    reduce_sum x2, other arithmetic, daily_score_parts(): jnp.sum(dvar * base_exp, axis=0)  9.22 us
  transfers between devices with their start and end apart: 10, of which 10 were waited for; matrix products, arithmetic and copies ran while one was open for 1% of the time, Pallas kernels for 0%

commit v1 on v0

v1 whole, which is shorter than its diff:
```python
import jax
import jax.numpy as jnp
from jax import lax
from jax.sharding import PartitionSpec as P

ITERS = 2
STEP = 0.5
SMOOTH = 0.03
Y = 4


def pairs(count, partner):
    return [(i, partner(i)) for i in range(count)]


def swap_low(i):
    return i ^ 1


def swap_high(i):
    return i ^ 3


def swap_z(i):
    return i ^ Y


def exchange(block, partner):
    return lax.ppermute(block, "tm", pairs(lax.axis_size("tm"), partner))


def day_sums(theta, fmean, fvar, obs):
    base_exp = jnp.exp(theta[2])
    spread = jnp.sqrt(base_exp + theta[3] * theta[3] * fvar)
    center = theta[0] + theta[1] * fmean
    standard = (obs - center) / spread
    cumulative = 0.5 * (1.0 + jax.scipy.special.erf(standard * 0.7071067811865476))
    density = jnp.exp(-0.5 * standard * standard) * 0.3989422804014327
    dcenter = 1.0 - 2.0 * cumulative
    dvar = (2.0 * density - 0.5641895835477563) / (2.0 * spread)
    return (
        jnp.sum(dcenter, axis=0),
        jnp.sum(dcenter * fmean, axis=0),
        jnp.sum(dvar * base_exp, axis=0),
        jnp.sum(dvar * 2.0 * theta[3] * fvar, axis=0),
    )


def laplace(extended):
    middle = extended[1:-1]
    along_lon = extended[2:] + extended[:-2] - 2.0 * middle
    steps = middle[:, 1:] - middle[:, :-1]
    zero = jnp.zeros((middle.shape[0], 1), jnp.float32)
    return along_lon + (
        jnp.concatenate([steps, zero], axis=1) - jnp.concatenate([zero, steps], axis=1)
    )


def smoothed(field):
    count = lax.axis_size("space")
    low = lax.ppermute(field[-2:], "space", pairs(count, lambda i: (i + 1) % count))
    high = lax.ppermute(field[:2], "space", pairs(count, lambda i: (i - 1) % count))
    extended = jnp.concatenate([low, field, high], axis=0)
    return field - (STEP * SMOOTH) * laplace(laplace(extended))


def on_device(fmean, fvar, obs, theta):
    days = fmean.shape[0] * lax.axis_size("tm")
    at_y = lax.axis_index("tm") % Y
    high = at_y // 2
    low = (at_y ^ high) % 2
    first_low, first_high = low == 0, high == 0
    mine = jnp.where(
        first_high, jnp.where(first_low, theta[0], theta[1]), jnp.where(first_low, theta[2], theta[3])
    )
    for _ in range(ITERS):
        base = smoothed(mine)
        s = day_sums(theta, fmean, fvar, obs)
        keep = [jnp.where(first_low, s[0], s[1]), jnp.where(first_low, s[2], s[3])]
        send = jnp.stack([jnp.where(first_low, s[1], s[0]), jnp.where(first_low, s[3], s[2])])
        got = exchange(send, swap_low)
        send = jnp.where(first_high, keep[1] + got[1], keep[0] + got[0])
        keep = jnp.where(first_high, keep[0] + got[0], keep[1] + got[1])
        total = keep + exchange(send, swap_high)
        total = total + exchange(total, swap_z)
        mine = base - (STEP / days) * total
        other = exchange(mine, swap_high)
        pair = jnp.stack([jnp.where(first_high, mine, other), jnp.where(first_high, other, mine)])
        across = exchange(pair, swap_low)
        theta = jnp.stack(
            [
                jnp.where(first_low, pair[0], across[0]),
                jnp.where(first_low, across[0], pair[0]),
                jnp.where(first_low, pair[1], across[1]),
                jnp.where(first_low, across[1], pair[1]),
            ]
        )
    return theta


def solution(mesh):
    days = P("tm", "space", None)
    fields = P(None, "space", None)
    return jax.shard_map(
        on_device,
        mesh=mesh,
        in_specs=(days, days, days, fields),
        out_specs=fields,
        check_vma=False,
    )
```

time: 271 us -> 131 us (0.48); the launches traced: 268 us -> 131 us
  waiting for transfers between devices: 213 us -> 74 us
  starting transfers between devices: 3.69 us -> 26.7 us
  between operations: 13.6 us -> 0.3 us
  other arithmetic: 31.7 us -> 24.6 us
    psum x2 -> x0, waiting for transfers between devices: 195 us -> none  [apply_update(): aggregate_loss = lax.psum(partial_sum, 'tm')]
    ppermute x8 -> x14, waiting for transfers between devices: 18.4 us -> 74 us  [the longest x10 64.1 us: exchange(): return lax.ppermute(block, 'tm', pairs(lax.axis_size('tm'), partner))]
    ppermute x8 -> x14, starting transfers between devices: 3.64 us -> 26.7 us  [the longest x10 24.7 us: exchange(): return lax.ppermute(block, 'tm', pairs(lax.axis_size('tm'), partner))]
    sub x8, other arithmetic: 16 us -> 10.8 us  [the longest x2 9.91 us: day_sums(): dcenter = 1.0 - 2.0 * cumulative]
    unnamed x9 -> x10, local copies, waits for them, and re-layouts: 3.26 us -> 0.43 us
  transfers between devices with their start and end apart: 10 -> 14, of which waited for: 10 -> 14; matrix products, arithmetic and copies ran while one was open for 1% -> 1% of each run, Pallas kernels for 0% -> 0%
where the time goes in v1:
time: 131 us
  waiting for transfers between devices  74 us (56%)
  starting transfers between devices  26.7 us (20%)
  other arithmetic  24.6 us (19%)
  local copies, waits for them, and re-layouts  5.34 us (4%)
    ppermute x10, waiting for transfers between devices, exchange(): return lax.ppermute(block, 'tm', pairs(lax.axis_size('tm'), partner))  64.1 us
    ppermute x10, starting transfers between devices, exchange(): return lax.ppermute(block, 'tm', pairs(lax.axis_size('tm'), partner))  24.7 us
    sub x2, other arithmetic, day_sums(): dcenter = 1.0 - 2.0 * cumulative  9.91 us
    reduce_sum x2, other arithmetic, day_sums(): jnp.sum(dvar * base_exp, axis=0)  9.23 us
    ppermute x2, waiting for transfers between devices, smoothed(): lax.ppermute(field[-2:], 'space', pairs(count, lambda i: (i + 1) % count))  7.66 us
    slice x1, local copies, waits for them, and re-layouts, on_device(): theta[1]  3.33 us
    reduce_sum x2, other arithmetic, day_sums(): jnp.sum(dcenter, axis=0)  3.3 us
  transfers between devices with their start and end apart: 14, of which 14 were waited for; matrix products, arithmetic and copies ran while one was open for 1% of the time, Pallas kernels for 0%

profile of v1, /device:TPU:64, one launch (start us, length us, event | category | flops | bytes accessed | tf_op | source)
XLA Modules:
  0.0 130.9 jit_solution(9093982071388277310)
XLA Ops:
  0.0 3.3 %fusion.36 = (f32[1,90,640]{2,0,1:T(1,128)S(1)}, f32[1,90,640]{2,0,1:T(1,128)S(1)}, f32[1,90,640]{2,0,1:T(1,128)S(1)}, f32[1,90,640]{2,0,1:T(1,128)S(1)}) fusion(f32[4,90,640]{2,0,1:T(4,128)} %param.7), kind=kLoop, calls=%fused_computation.97 | loop fusion | bytes 1843200 | tf_op jit(solution)/shard_map/slice | solution.py:74
  3.3 0.1 multiply_bitcast_fusion
  3.4 0.1 copy_bitcast_fusion
  3.5 0.0 copy-start
  3.5 6.8 %add_subtract_fusion.1 = (f32[16,90,640]{2,0,1:T(8,128)S(1)}, f32[16,90,640]{2,0,1:T(8,128)S(1)}) fusion(f32[16,90,640]{2,0,1:T(8,128)} %param.5, f32[90,640]{1,0:T(8,128)S(1)} %get-tuple-element.49, f32[90,640]{1,0:T(8,128)S(1)} %get-tuple-element.52, f32[16,90,640]{2,0,1:T(8,128)} %param.6, f32[16,90,640]{2,0,1:T(8,128)} %param.4, ...), kind=kLoop, calls=%fused_computation.19 | loop fusion | flops 8294400 | bytes 19353600 | tf_op jit(solution)/shard_map/sub | solution.py:39
  10.3 0.0 copy-done
  10.3 0.0 copy-start.2
  10.3 1.6 %fusion.31 = (f32[90,640]{1,0:T(8,128)S(1)}, f32[90,640]{1,0:T(8,128)S(1)}) fusion(f32[16,90,640]{2,0,1:T(8,128)S(1)} %get-tuple-element.21, f32[16,90,640]{2,0,1:T(8,128)S(1)} %copy-done), kind=kLoop, calls=%fused_computation.96 | loop fusion | flops 2649600 | bytes 7833600 | tf_op jit(solution)/shard_map/reduce_sum | solution.py:42
  12.0 0.4 copy-done.2
  12.4 4.6 %multiply_reduce_fusion.3 = (f32[90,640]{1,0:T(8,128)S(1)}, f32[90,640]{1,0:T(8,128)S(1)}) fusion(f32[90,640]{1,0:T(8,128)S(1)} %get-tuple-element.52, f32[16,90,640]{2,0,1:T(8,128)S(1)} %copy-done.2, f32[90,640]{1,0:T(8,128)S(1)} %get-tuple-element.49, f32[16,90,640]{2,0,1:T(8,128)S(1)} %get-tuple-element.22, f32[90,640]{1,0:T(8,128)S(1)} %get-tuple-element.48), kind=kLoop, calls=%fused_computation.16 | loop fusion | flops 11865600 | bytes 8524800 | tf_op jit(solution)/shard_map/reduce_sum | solution.py:44
  17.1 1.7 %collective-permute-start.2 = (f32[2,90,640]{2,1,0:T(8,128)S(1)}, f32[2,90,640]{2,1,0:T(8,128)S(1)}, u32[]{:S(2)}, u32[]{:S(2)}) collective-permute-start(f32[2,90,640]{2,1,0:T(8,128)S(1)} %pad_maximum_fusion.1), channel_id=1, source_target_pairs={{0,32},{32,0},{64,96},{96,64},{128,160},{160,128},{192,224},{224,1... | collective-permute-start | bytes 1382408 | tf_op jit(solution)/shard_map/ppermute | solution.py:29
  18.8 0.1 bitcast_select_fusion
  18.9 1.5 %collective-permute-start = (f32[2,640]{1,0:T(2,128)S(1)}, f32[2,640]{1,0:T(2,128)S(1)}, u32[]{:S(2)}, u32[]{:S(2)}) collective-permute-start(f32[2,640]{1,0:T(2,128)S(1)} %get-tuple-element.47), channel_id=1, source_target_pairs={{0,31},{1,0},{2,1},{3,2},{4,3},{5,4},{6,5},{7,6},{8,7},{9,8},{10,9... | collective-permute-start | bytes 15368 | tf_op jit(solution)/shard_map/ppermute | solution.py:62
  20.4 0.0 collective-permute-start.1
  20.4 1.3 %collective-permute-done = f32[2,640]{1,0:T(2,128)S(1)} collective-permute-done((f32[2,640]{1,0:T(2,128)S(1)}, f32[2,640]{1,0:T(2,128)S(1)}, u32[]{:S(2)}, u32[]{:S(2)}) %collective-permute-start) | collective-permute-done | bytes 5152 | tf_op jit(solution)/shard_map/ppermute | solution.py:62
  21.7 3.8 %collective-permute-done.1 = f32[2,640]{1,0:T(2,128)S(1)} collective-permute-done((f32[2,640]{1,0:T(2,128)S(1)}, f32[2,640]{1,0:T(2,128)S(1)}, u32[]{:S(2)}, u32[]{:S(2)}) %collective-permute-start.1) | collective-permute-done | bytes 5152 | tf_op jit(solution)/shard_map/ppermute | solution.py:61
  25.6 0.1 slice_subtract_fusion.3
  25.7 4.4 %collective-permute-done.2 = f32[2,90,640]{2,1,0:T(8,128)S(1)} collective-permute-done((f32[2,90,640]{2,1,0:T(8,128)S(1)}, f32[2,90,640]{2,1,0:T(8,128)S(1)}, u32[]{:S(2)}, u32[]{:S(2)}) %collective-permute-start.2) | collective-permute-done | bytes 460832 | tf_op jit(solution)/shard_map/ppermute | solution.py:29
  30.2 0.0 copy-start.4
  30.2 0.1 broadcast_select_fusion.5
  30.2 3.1 %collective-permute-start.3 = (f32[90,640]{1,0:T(8,128)S(1)}, f32[90,640]{1,0:T(8,128)S(1)}, u32[]{:S(2)}, u32[]{:S(2)}) collective-permute-start(f32[90,640]{1,0:T(8,128)S(1)} %get-tuple-element.18), channel_id=1, source_target_pairs={{0,96},{32,64},{64,32},{96,0},{128,224},{160,192},{192,160},{224,1... | collective-permute-start | bytes 691208 | tf_op jit(solution)/shard_map/ppermute | solution.py:29
  33.3 0.1 fusion.25
  33.5 5.0 %collective-permute-done.3 = f32[90,640]{1,0:T(8,128)S(1)} collective-permute-done((f32[90,640]{1,0:T(8,128)S(1)}, f32[90,640]{1,0:T(8,128)S(1)}, u32[]{:S(2)}, u32[]{:S(2)}) %collective-permute-start.3) | collective-permute-done | bytes 230432 | tf_op jit(solution)/shard_map/ppermute | solution.py:29
  38.4 0.0 copy-start.3
  38.5 0.0 copy-start.1
  38.5 5.5 %collective-permute-start.4 = (f32[90,640]{1,0:T(8,128)S(1)}, f32[90,640]{1,0:T(8,128)S(1)}, u32[]{:S(2)}, u32[]{:S(2)}) collective-permute-start(f32[90,640]{1,0:T(8,128)S(1)} %select_add_fusion.1), channel_id=1, source_target_pairs={{0,128},{32,160},{64,192},{96,224},{128,0},{160,32},{192,64},{224,... | collective-permute-start | bytes 691208 | tf_op jit(solution)/shard_map/ppermute | solution.py:29
  44.0 0.1 slice_subtract_fusion.2
  44.1 9.8 %collective-permute-done.4 = f32[90,640]{1,0:T(8,128)S(1)} collective-permute-done((f32[90,640]{1,0:T(8,128)S(1)}, f32[90,640]{1,0:T(8,128)S(1)}, u32[]{:S(2)}, u32[]{:S(2)}) %collective-permute-start.4) | collective-permute-done | bytes 230432 | tf_op jit(solution)/shard_map/ppermute | solution.py:29
  53.9 0.2 fusion.23
  54.1 3.0 %collective-permute-start.7 = (f32[90,640]{1,0:T(8,128)S(1)}, f32[90,640]{1,0:T(8,128)S(1)}, u32[]{:S(2)}, u32[]{:S(2)}) collective-permute-start(f32[90,640]{1,0:T(8,128)S(1)} %fusion.23), channel_id=1, source_target_pairs={{0,96},{32,64},{64,32},{96,0},{128,224},{160,192},{192,160},{224,1... | collective-permute-start | bytes 691208 | tf_op jit(solution)/shard_map/ppermute | solution.py:29
  57.1 5.4 %collective-permute-done.7 = f32[90,640]{1,0:T(8,128)S(1)} collective-permute-done((f32[90,640]{1,0:T(8,128)S(1)}, f32[90,640]{1,0:T(8,128)S(1)}, u32[]{:S(2)}, u32[]{:S(2)}) %collective-permute-start.7) | collective-permute-done | bytes 230432 | tf_op jit(solution)/shard_map/ppermute | solution.py:29
  62.6 0.3 collective-permute-start.8
  62.9 11.5 %collective-permute-done.8 = f32[2,90,640]{2,1,0:T(8,128)S(1)} collective-permute-done((f32[2,90,640]{2,1,0:T(8,128)S(1)}, f32[2,90,640]{2,1,0:T(8,128)S(1)}, u32[]{:S(2)}, u32[]{:S(2)}) %collective-permute-start.8) | collective-permute-done | bytes 460832 | tf_op jit(solution)/shard_map/ppermute | solution.py:29
  74.4 0.1 broadcast_multiply_fusion
  74.5 0.0 copy-done.4
  74.5 0.0 copy-done.3
  74.5 0.0 copy-done.1
  74.5 3.1 %add_subtract_fusion = (f32[16,90,640]{2,0,1:T(8,128)S(1)}, f32[16,90,640]{2,0,1:T(8,128)S(1)}) fusion(f32[16,90,640]{2,0,1:T(8,128)S(1)} %copy-done.3, f32[90,640]{1,0:T(8,128)S(1)} %get-tuple-element.32, f32[90,640]{1,0:T(8,128)S(1)} %get-tuple-element.33, f32[16,90,640]{2,0,1:T(8,128)S(1)} %copy-done.4, f32[16,90,640]{2,0,1:T(8,128)S(1)} %copy-done.1, ...), kind=kLoop, calls=%fused_computation.13 | loop fusion | flops 8294400 | bytes 19353600 | tf_op jit(solution)/shard_map/sub | solution.py:39
  77.6 1.7 %fusion.30 = (f32[90,640]{1,0:T(8,128)S(1)}, f32[90,640]{1,0:T(8,128)S(1)}) fusion(f32[16,90,640]{2,0,1:T(8,128)S(1)} %get-tuple-element.16, f32[16,90,640]{2,0,1:T(8,128)S(1)} %copy-done.1), kind=kLoop, calls=%fused_computation.95 | loop fusion | flops 2649600 | bytes 7833600 | tf_op jit(solution)/shard_map/reduce_sum | solution.py:42
  79.3 4.6 %multiply_reduce_fusion = (f32[90,640]{1,0:T(8,128)S(1)}, f32[90,640]{1,0:T(8,128)S(1)}) fusion(f32[90,640]{1,0:T(8,128)S(1)} %get-tuple-element.33, f32[16,90,640]{2,0,1:T(8,128)S(1)} %copy-done.3, f32[90,640]{1,0:T(8,128)S(1)} %get-tuple-element.32, f32[16,90,640]{2,0,1:T(8,128)S(1)} %get-tuple-element.17, f32[90,640]{1,0:T(8,128)S(1)} %get-tuple-element.31), kind=kLoop, calls=%fused_computation.10 | loop fusion | flops 11865600 | bytes 8524800 | tf_op jit(solution)/shard_map/reduce_sum | solution.py:44
  84.0 0.4 collective-permute-start.9
  84.4 0.0 collective-permute-start.5
  84.4 0.5 collective-permute-start.6
  84.9 0.8 collective-permute-done.5
  85.7 3.8 %collective-permute-done.6 = f32[2,640]{1,0:T(2,128)S(1)} collective-permute-done((f32[2,640]{1,0:T(2,128)S(1)}, f32[2,640]{1,0:T(2,128)S(1)}, u32[]{:S(2)}, u32[]{:S(2)}) %collective-permute-start.6) | collective-permute-done | bytes 5152 | tf_op jit(solution)/shard_map/ppermute | solution.py:61
  89.6 0.1 slice_subtract_fusion.1
  89.7 5.0 %collective-permute-done.9 = f32[2,90,640]{2,1,0:T(8,128)S(1)} collective-permute-done((f32[2,90,640]{2,1,0:T(8,128)S(1)}, f32[2,90,640]{2,1,0:T(8,128)S(1)}, u32[]{:S(2)}, u32[]{:S(2)}) %collective-permute-start.9) | collective-permute-done | bytes 460832 | tf_op jit(solution)/shard_map/ppermute | solution.py:29
  94.8 0.1 broadcast_select_fusion.2
  94.8 3.0 %collective-permute-start.10 = (f32[90,640]{1,0:T(8,128)S(1)}, f32[90,640]{1,0:T(8,128)S(1)}, u32[]{:S(2)}, u32[]{:S(2)}) collective-permute-start(f32[90,640]{1,0:T(8,128)S(1)} %get-tuple-element.13), channel_id=1, source_target_pairs={{0,96},{32,64},{64,32},{96,0},{128,224},{160,192},{192,160},{224,1... | collective-permute-start | bytes 691208 | tf_op jit(solution)/shard_map/ppermute | solution.py:29
  97.8 0.1 fusion.16
  98.0 4.4 %collective-permute-done.10 = f32[90,640]{1,0:T(8,128)S(1)} collective-permute-done((f32[90,640]{1,0:T(8,128)S(1)}, f32[90,640]{1,0:T(8,128)S(1)}, u32[]{:S(2)}, u32[]{:S(2)}) %collective-permute-start.10) | collective-permute-done | bytes 230432 | tf_op jit(solution)/shard_map/ppermute | solution.py:29
  102.4 4.8 %collective-permute-start.11 = (f32[90,640]{1,0:T(8,128)S(1)}, f32[90,640]{1,0:T(8,128)S(1)}, u32[]{:S(2)}, u32[]{:S(2)}) collective-permute-start(f32[90,640]{1,0:T(8,128)S(1)} %select_add_fusion), channel_id=1, source_target_pairs={{0,128},{32,160},{64,192},{96,224},{128,0},{160,32},{192,64},{224,... | collective-permute-start | bytes 691208 | tf_op jit(solution)/shard_map/ppermute | solution.py:29
  107.1 0.1 slice_subtract_fusion
  107.3 5.3 %collective-permute-done.11 = f32[90,640]{1,0:T(8,128)S(1)} collective-permute-done((f32[90,640]{1,0:T(8,128)S(1)}, f32[90,640]{1,0:T(8,128)S(1)}, u32[]{:S(2)}, u32[]{:S(2)}) %collective-permute-start.11) | collective-permute-done | bytes 230432 | tf_op jit(solution)/shard_map/ppermute | solution.py:29
  112.6 0.2 fusion.14
  112.8 3.0 %collective-permute-start.12 = (f32[90,640]{1,0:T(8,128)S(1)}, f32[90,640]{1,0:T(8,128)S(1)}, u32[]{:S(2)}, u32[]{:S(2)}) collective-permute-start(f32[90,640]{1,0:T(8,128)S(1)} %fusion.14), channel_id=1, source_target_pairs={{0,96},{32,64},{64,32},{96,0},{128,224},{160,192},{192,160},{224,1... | collective-permute-start | bytes 691208 | tf_op jit(solution)/shard_map/ppermute | solution.py:29
  115.7 4.5 %collective-permute-done.12 = f32[90,640]{1,0:T(8,128)S(1)} collective-permute-done((f32[90,640]{1,0:T(8,128)S(1)}, f32[90,640]{1,0:T(8,128)S(1)}, u32[]{:S(2)}, u32[]{:S(2)}) %collective-permute-start.12) | collective-permute-done | bytes 230432 | tf_op jit(solution)/shard_map/ppermute | solution.py:29
  120.3 0.1 broadcast_select_fusion.1
  120.4 0.1 collective-permute-start.13
  120.5 8.8 %collective-permute-done.13 = f32[2,90,640]{2,1,0:T(8,128)S(1)} collective-permute-done((f32[2,90,640]{2,1,0:T(8,128)S(1)}, f32[2,90,640]{2,1,0:T(8,128)S(1)}, u32[]{:S(2)}, u32[]{:S(2)}) %collective-permute-start.13) | collective-permute-done | bytes 460832 | tf_op jit(solution)/shard_map/ppermute | solution.py:29
  129.3 0.1 select_bitcast_fusion.3
  129.3 0.1 pad_maximum_fusion
  129.4 1.5 %copy.16 = f32[4,90,640]{2,0,1:T(4,128)} copy(f32[4,90,640]{2,1,0:T(8,128)S(1)} %pad_maximum_fusion) | data formatting | bytes 1843200 | tf_op jit(solution)/shard_map/stack | solution.py:90
  (15 shorter events, 0.4 us)
Async XLA Ops:
  3.5 6.8 %copy-start = (f32[16,90,640]{2,0,1:T(8,128)S(1)}, f32[16,90,640]{2,0,1:T(8,128)}, u32[]{:S(2)}) copy-start(f32[16,90,640]{2,0,1:T(8,128)} %param.4) | copy-start | bytes 11059204
  10.3 2.0 %copy-start.2 = (f32[16,90,640]{2,0,1:T(8,128)S(1)}, f32[16,90,640]{2,0,1:T(8,128)}, u32[]{:S(2)}) copy-start(f32[16,90,640]{2,0,1:T(8,128)} %param.5) | copy-start | bytes 11059204
  17.1 13.0 %collective-permute-start.2 = (f32[2,90,640]{2,1,0:T(8,128)S(1)}, f32[2,90,640]{2,1,0:T(8,128)S(1)}, u32[]{:S(2)}, u32[]{:S(2)}) collective-permute-start(f32[2,90,640]{2,1,0:T(8,128)S(1)} %pad_maximum_fusion.1), channel_id=1, source_target_pairs={{0,32},{32,0},{64,96},{96,64},{128,160},{160,128},{192,224},{224,1... | collective-permute-start | bytes 1382408 | tf_op jit(solution)/shard_map/ppermute | solution.py:29
  18.9 2.9 %collective-permute-start = (f32[2,640]{1,0:T(2,128)S(1)}, f32[2,640]{1,0:T(2,128)S(1)}, u32[]{:S(2)}, u32[]{:S(2)}) collective-permute-start(f32[2,640]{1,0:T(2,128)S(1)} %get-tuple-element.47), channel_id=1, source_target_pairs={{0,31},{1,0},{2,1},{3,2},{4,3},{5,4},{6,5},{7,6},{8,7},{9,8},{10,9... | collective-permute-start | bytes 15368 | tf_op jit(solution)/shard_map/ppermute | solution.py:62
  20.4 5.2 %collective-permute-start.1 = (f32[2,640]{1,0:T(2,128)S(1)}, f32[2,640]{1,0:T(2,128)S(1)}, u32[]{:S(2)}, u32[]{:S(2)}) collective-permute-start(f32[2,640]{1,0:T(2,128)S(1)} %get-tuple-element.46), channel_id=1, source_target_pairs={{0,1},{1,2},{2,3},{3,4},{4,5},{5,6},{6,7},{7,8},{8,9},{9,10},{10,1... | collective-permute-start | bytes 15368 | tf_op jit(solution)/shard_map/ppermute | solution.py:61
  30.2 44.3 %copy-start.4 = (f32[16,90,640]{2,0,1:T(8,128)S(1)}, f32[16,90,640]{2,0,1:T(8,128)}, u32[]{:S(2)}) copy-start(f32[16,90,640]{2,0,1:T(8,128)} %param.6) | copy-start | bytes 11059204
  30.2 8.2 %collective-permute-start.3 = (f32[90,640]{1,0:T(8,128)S(1)}, f32[90,640]{1,0:T(8,128)S(1)}, u32[]{:S(2)}, u32[]{:S(2)}) collective-permute-start(f32[90,640]{1,0:T(8,128)S(1)} %get-tuple-element.18), channel_id=1, source_target_pairs={{0,96},{32,64},{64,32},{96,0},{128,224},{160,192},{192,160},{224,1... | collective-permute-start | bytes 691208 | tf_op jit(solution)/shard_map/ppermute | solution.py:29
  38.4 36.1 %copy-start.3 = (f32[16,90,640]{2,0,1:T(8,128)S(1)}, f32[16,90,640]{2,0,1:T(8,128)}, u32[]{:S(2)}) copy-start(f32[16,90,640]{2,0,1:T(8,128)} %param.5) | copy-start | bytes 11059204
  38.5 36.0 %copy-start.1 = (f32[16,90,640]{2,0,1:T(8,128)S(1)}, f32[16,90,640]{2,0,1:T(8,128)}, u32[]{:S(2)}) copy-start(f32[16,90,640]{2,0,1:T(8,128)} %param.4) | copy-start | bytes 11059204
  38.5 15.4 %collective-permute-start.4 = (f32[90,640]{1,0:T(8,128)S(1)}, f32[90,640]{1,0:T(8,128)S(1)}, u32[]{:S(2)}, u32[]{:S(2)}) collective-permute-start(f32[90,640]{1,0:T(8,128)S(1)} %select_add_fusion.1), channel_id=1, source_target_pairs={{0,128},{32,160},{64,192},{96,224},{128,0},{160,32},{192,64},{224,... | collective-permute-start | bytes 691208 | tf_op jit(solution)/shard_map/ppermute | solution.py:29
  54.1 8.4 %collective-permute-start.7 = (f32[90,640]{1,0:T(8,128)S(1)}, f32[90,640]{1,0:T(8,128)S(1)}, u32[]{:S(2)}, u32[]{:S(2)}) collective-permute-start(f32[90,640]{1,0:T(8,128)S(1)} %fusion.23), channel_id=1, source_target_pairs={{0,96},{32,64},{64,32},{96,0},{128,224},{160,192},{192,160},{224,1... | collective-permute-start | bytes 691208 | tf_op jit(solution)/shard_map/ppermute | solution.py:29
  62.6 11.8 %collective-permute-start.8 = (f32[2,90,640]{2,1,0:T(8,128)S(1)}, f32[2,90,640]{2,1,0:T(8,128)S(1)}, u32[]{:S(2)}, u32[]{:S(2)}) collective-permute-start(f32[2,90,640]{2,1,0:T(8,128)S(1)} %pad_maximum_fusion.2), channel_id=1, source_target_pairs={{0,32},{32,0},{64,96},{96,64},{128,160},{160,128},{192,224},{224,1... | collective-permute-start | bytes 1382408 | tf_op jit(solution)/shard_map/ppermute | solution.py:29
  84.0 10.7 %collective-permute-start.9 = (f32[2,90,640]{2,1,0:T(8,128)S(1)}, f32[2,90,640]{2,1,0:T(8,128)S(1)}, u32[]{:S(2)}, u32[]{:S(2)}) collective-permute-start(f32[2,90,640]{2,1,0:T(8,128)S(1)} %pad_maximum_fusion.3), channel_id=1, source_target_pairs={{0,32},{32,0},{64,96},{96,64},{128,160},{160,128},{192,224},{224,1... | collective-permute-start | bytes 1382408 | tf_op jit(solution)/shard_map/ppermute | solution.py:29
  84.4 1.3 %collective-permute-start.5 = (f32[2,640]{1,0:T(2,128)S(1)}, f32[2,640]{1,0:T(2,128)S(1)}, u32[]{:S(2)}, u32[]{:S(2)}) collective-permute-start(f32[2,640]{1,0:T(2,128)S(1)} %get-tuple-element.45), channel_id=1, source_target_pairs={{0,31},{1,0},{2,1},{3,2},{4,3},{5,4},{6,5},{7,6},{8,7},{9,8},{10,9... | collective-permute-start | bytes 15368 | tf_op jit(solution)/shard_map/ppermute | solution.py:62
  84.4 5.2 %collective-permute-start.6 = (f32[2,640]{1,0:T(2,128)S(1)}, f32[2,640]{1,0:T(2,128)S(1)}, u32[]{:S(2)}, u32[]{:S(2)}) collective-permute-start(f32[2,640]{1,0:T(2,128)S(1)} %get-tuple-element.44), channel_id=1, source_target_pairs={{0,1},{1,2},{2,3},{3,4},{4,5},{5,6},{6,7},{7,8},{8,9},{9,10},{10,1... | collective-permute-start | bytes 15368 | tf_op jit(solution)/shard_map/ppermute | solution.py:61
  94.8 7.5 %collective-permute-start.10 = (f32[90,640]{1,0:T(8,128)S(1)}, f32[90,640]{1,0:T(8,128)S(1)}, u32[]{:S(2)}, u32[]{:S(2)}) collective-permute-start(f32[90,640]{1,0:T(8,128)S(1)} %get-tuple-element.13), channel_id=1, source_target_pairs={{0,96},{32,64},{64,32},{96,0},{128,224},{160,192},{192,160},{224,1... | collective-permute-start | bytes 691208 | tf_op jit(solution)/shard_map/ppermute | solution.py:29
  102.4 10.2 %collective-permute-start.11 = (f32[90,640]{1,0:T(8,128)S(1)}, f32[90,640]{1,0:T(8,128)S(1)}, u32[]{:S(2)}, u32[]{:S(2)}) collective-permute-start(f32[90,640]{1,0:T(8,128)S(1)} %select_add_fusion), channel_id=1, source_target_pairs={{0,128},{32,160},{64,192},{96,224},{128,0},{160,32},{192,64},{224,... | collective-permute-start | bytes 691208 | tf_op jit(solution)/shard_map/ppermute | solution.py:29
  112.8 7.5 %collective-permute-start.12 = (f32[90,640]{1,0:T(8,128)S(1)}, f32[90,640]{1,0:T(8,128)S(1)}, u32[]{:S(2)}, u32[]{:S(2)}) collective-permute-start(f32[90,640]{1,0:T(8,128)S(1)} %fusion.14), channel_id=1, source_target_pairs={{0,96},{32,64},{64,32},{96,0},{128,224},{160,192},{192,160},{224,1... | collective-permute-start | bytes 691208 | tf_op jit(solution)/shard_map/ppermute | solution.py:29
  120.4 8.9 %collective-permute-start.13 = (f32[2,90,640]{2,1,0:T(8,128)S(1)}, f32[2,90,640]{2,1,0:T(8,128)S(1)}, u32[]{:S(2)}, u32[]{:S(2)}) collective-permute-start(f32[2,90,640]{2,1,0:T(8,128)S(1)} %pad_maximum_fusion.4), channel_id=1, source_target_pairs={{0,32},{32,0},{64,96},{96,64},{128,160},{160,128},{192,224},{224,1... | collective-permute-start | bytes 1382408 | tf_op jit(solution)/shard_map/ppermute | solution.py:29

commit v2 on v1

v2 whole, which is shorter than its diff:
```python
import functools

import jax
import jax.numpy as jnp
from jax import lax
from jax.experimental import pallas as pl
from jax.experimental.pallas import tpu as pltpu
from jax.sharding import PartitionSpec as P


ITERS = 2
STEP = 0.5
SMOOTH = 0.03
Y = 4
ORDER = (2, 1, 3, 0)
GROUP = 4

BEND = 0.33
TAIL = (
    0.24258075161877687,
    0.4135445348314681,
    -0.19449665181676495,
    0.7602243169976308,
    -0.22185304956855628,
)
UNIT = (-TAIL[4]) ** 0.2
TAIL_UNIT = tuple(c / UNIT ** (i + 1) for i, c in enumerate(TAIL[:4]))
GAUGE = BEND / UNIT
POWER = -0.7213475204444817 / GAUGE**2
LEVEL = 0.7071067811865476
DENSITY = 0.3989422804014327
FACTORS = (1.0, 1.0, DENSITY * GAUGE, 2.0 * DENSITY / GAUGE)


def tall_of(rows):
    return -(-rows // Y)


def first_of(which, rows):
    return jnp.minimum(which * tall_of(rows), rows - tall_of(rows))


def sum_row(theta_ref, m_ref, v_ref, o_ref, out_ref, row):
    days, columns = m_ref.shape[1:]
    for j in range(columns // 128):
        lanes = slice(128 * j, 128 * j + 128)
        a, b, c, d = [
            jnp.broadcast_to(theta_ref[row, f : f + 1, lanes], (8, 128)) for f in range(4)
        ]
        base, slope = jnp.exp(c) * GAUGE**-2, d * d * GAUGE**-2
        sums = None
        for i in range(days // 8):
            at = slice(8 * i, 8 * i + 8)
            m, v, o = m_ref[row, at, lanes], v_ref[row, at, lanes], o_ref[row, at, lanes]
            r = lax.rsqrt(base + slope * v)
            z = ((o - a) - b * m) * r
            q = jnp.exp2((z * z) * POWER)
            k = 1.0 / (1.0 / UNIT + jnp.abs(z))
            tail = TAIL_UNIT[3] - k
            for coefficient in TAIL_UNIT[2::-1]:
                tail = tail * k + coefficient
            g = (tail * k) * q - 1.0
            g = jnp.where(z < 0.0, -g, g)
            h = (q - LEVEL) * r
            terms = [g, g * m, h, h * v]
            sums = terms if sums is None else [s + t for s, t in zip(sums, terms)]
        sums = [jnp.sum(s, axis=0, keepdims=True) for s in sums]
        sums = [sums[0], sums[1], sums[2] * base[:1], sums[3] * d[:1]]
        for f in range(4):
            out_ref[row, f : f + 1, lanes] = sums[f]


def sum_rows(refs, ready=None):
    tall = refs[-1].shape[0]
    turns = tall // GROUP

    def turn(i, carry):
        if ready is not None:
            ready(i * GROUP, GROUP, i)
        for n in range(GROUP):
            sum_row(*refs, i * GROUP + n)
        return carry

    lax.fori_loop(0, turns, turn, 0)
    if tall % GROUP:
        if ready is not None:
            ready(turns * GROUP, tall % GROUP, turns)
        for n in range(turns * GROUP, tall):
            sum_row(*refs, n)


def quarter_copies(at_y, k, sources, targets, sems):
    rows, tall = sources[0].shape[0], targets[0].shape[0]
    first = first_of((at_y[0] + k) % Y, rows)

    def group(start, size, i):
        return [
            pltpu.make_async_copy(
                s.at[pl.ds(first + start, size)], t.at[pl.ds(start, size)], sems.at[i, n]
            )
            for n, (s, t) in enumerate(zip(sources, targets))
        ]

    every = [group(g, min(GROUP, tall - g), g // GROUP) for g in range(0, tall, GROUP)]
    return group, every


def start_all(groups):
    for group in groups:
        for copy in group:
            copy.start()


def wait_all(groups):
    for group in groups:
        for copy in group:
            copy.wait()


def first_kernel(at_y, *refs):
    whole, out_ref, own, ahead = refs[:4], refs[4], refs[5:9], refs[9:13]
    sems, later_sems = refs[13:]
    group, every = quarter_copies(at_y, ORDER[0], whole, own, sems)
    later = quarter_copies(at_y, ORDER[1], whole, ahead, later_sems)[1]
    start_all(every)
    start_all(later)
    sum_rows((own[3], *own[:3], out_ref), lambda *rows: wait_all([group(*rows)]))
    wait_all(later)


def next_kernel(k, at_y, *refs):
    whole, own, out_ref, ahead, sems = refs[:4], refs[4:8], refs[8], refs[9:13], refs[13]
    every = quarter_copies(at_y, k, whole, ahead, sems)[1]
    start_all(every)
    sum_rows((own[3], *own[:3], out_ref))
    wait_all(every)


def last_kernel(*refs):
    sum_rows(refs)


def join_kernel(at_y, *refs):
    pieces, out_ref, sems = refs[:Y], refs[Y], refs[Y + 1]
    rows, tall = out_ref.shape[0], pieces[0].shape[0]
    shorter = rows - (Y - 1) * tall
    for go in (True, False):
        for k in range(Y):
            which = (at_y[0] + k) % Y

            @pl.when(which != Y - 2)
            def _(k=k, which=which):
                at = out_ref.at[pl.ds(first_of(which, rows), tall)]
                copy = pltpu.make_async_copy(pieces[k], at, sems.at[k])
                copy.start() if go else copy.wait()

            @pl.when(which == Y - 2)
            def _(k=k):
                at = out_ref.at[pl.ds((Y - 2) * tall, shorter)]
                copy = pltpu.make_async_copy(pieces[k].at[pl.ds(0, shorter)], at, sems.at[k])
                copy.start() if go else copy.wait()


SMEM = pl.BlockSpec(memory_space=pltpu.SMEM)
VMEM = pl.BlockSpec(memory_space=pltpu.VMEM)
HBM = pl.BlockSpec(memory_space=pltpu.HBM)


def call(kernel, inputs, in_specs, shapes, sems=()):
    size = 1
    for n in shapes[0]:
        size *= n
    cells = size // 4 * 16
    inputs = [
        pltpu.with_memory_space_constraint(x, spec.memory_space) if spec is not SMEM else x
        for x, spec in zip(inputs, in_specs)
    ]
    return pl.pallas_call(
        kernel,
        in_specs=in_specs,
        out_specs=[VMEM] * len(shapes),
        out_shape=[pltpu.VMEM(shape, jnp.float32) for shape in shapes],
        scratch_shapes=[pltpu.SemaphoreType.DMA(s) for s in sems],
        cost_estimate=pl.CostEstimate(flops=40 * cells, transcendentals=3 * cells, bytes_accessed=12 * cells),
        compiler_params=pltpu.CompilerParams(vmem_limit_bytes=4 << 20),
    )(*inputs)


def first_sums(at_y, whole):
    rows, days, columns = whole[0].shape
    tall = tall_of(rows)
    field = (tall, 4, columns)
    quarter = [(tall, days, columns)] * 3 + [field]
    sums, *rest = call(
        first_kernel,
        (at_y, *whole),
        [SMEM] + [HBM] * 4,
        [field] + quarter * 2,
        [(pl.cdiv(tall, GROUP), 4)] * 2,
    )
    own, ahead = rest[:4], rest[4:]
    yield ORDER[0], own[:3], own[3], sums
    for i in (1, 2):
        own = ahead
        sums, *ahead = call(
            functools.partial(next_kernel, ORDER[i + 1]),
            (at_y, *whole, *own),
            [SMEM] + [HBM] * 4 + [VMEM] * 4,
            [field] + quarter,
            [(pl.cdiv(tall, GROUP), 4)],
        )
        yield ORDER[i], own[:3], own[3], sums
    yield ORDER[3], ahead[:3], ahead[3], later_sums(ahead[:3], ahead[3])


def gathered(mine, shifts):
    pieces = {0: mine}
    for k in (2, 1, 3):
        pieces[k] = shift_y(mine, -shifts[k])
    return pieces


def later_steps(data, pieces):
    for k in (0, 2, 1, 3):
        yield k, data[k], pieces[k], later_sums(data[k], pieces[k])


def later_sums(data, theta):
    return call(last_kernel, (theta, *data), [VMEM] * 4, [theta.shape])[0]


def join(at_y, pieces, rows):
    return pl.pallas_call(
        join_kernel,
        in_specs=[SMEM] + [VMEM] * Y,
        out_specs=HBM,
        out_shape=jax.ShapeDtypeStruct((rows, *pieces[0].shape[1:]), jnp.float32),
        scratch_shapes=[pltpu.SemaphoreType.DMA((Y,))],
        compiler_params=pltpu.CompilerParams(vmem_limit_bytes=4 << 20),
        name="join",
    )(at_y, *pieces)


def shift_y(block, by):
    count = lax.axis_size("tm")
    return lax.ppermute(block, "tm", [(i, i // Y * Y + (i + by) % Y) for i in range(count)])


def swap_z(block):
    return lax.ppermute(block, "tm", [(i, i ^ Y) for i in range(lax.axis_size("tm"))])


def halo(flags, pieces):
    send = jnp.where(flags["first"], pieces[3][-2:], pieces[1][:2])
    groups, count = lax.axis_size("tm") // Y, lax.axis_size("space")
    pairs = []
    for g in range(groups):
        for s in range(count):
            over = (g + s // (count - 1)) % groups
            pairs.append(((g * Y) * count + s, over * Y * count + (s + 1) % count))
            pairs.append((((over + 1) * Y - 1) * count + (s + 1) % count, ((g + 1) * Y - 1) * count + s))
    return lax.ppermute(send, ("tm", "space"), pairs)


def laplace(extended):
    middle = extended[1:-1]
    along_lon = extended[2:] + extended[:-2] - 2.0 * middle
    steps = middle[..., 1:] - middle[..., :-1]
    zero = jnp.zeros(middle.shape[:2] + (1,), jnp.float32)
    return along_lon + (
        jnp.concatenate([steps, zero], axis=2) - jnp.concatenate([zero, steps], axis=2)
    )


def smoothed(flags, mine, below, above, edge, rows):
    shared = Y * mine.shape[0] - rows
    tall = mine.shape[0]
    low = jnp.where(flags["last"], below[tall - shared - 2 : tall - shared], below[-2:])
    low = jnp.where(flags["first"], edge, low)
    high = jnp.where(flags["third"], above[shared : shared + 2], above[:2])
    high = jnp.where(flags["last"], edge, high)
    return mine - (STEP * SMOOTH) * laplace(laplace(jnp.concatenate([low, mine, high])))


def on_device(fmean, fvar, obs, theta):
    days, rows, _ = fmean.shape
    scale = jnp.array(FACTORS, jnp.float32).reshape(1, 4, 1) * (STEP / (days * lax.axis_size("tm")))
    y = lax.axis_index("tm") % Y
    at_y = jnp.reshape(y, (1,)).astype(jnp.int32)
    flags = {"first": y == 0, "third": y == Y - 2, "last": y == Y - 1}
    at_y, flags = lax.optimization_barrier((at_y, flags))
    whole = [jnp.transpose(x, (1, 0, 2)) for x in (fmean, fvar, obs, theta)]
    shifts = {1: 1, 2: 2, 3: -1}
    data, pieces = {}, {}
    for step in range(ITERS):
        if step:
            pieces = gathered(mine, shifts)
            made = later_steps(data, pieces)
        else:
            made = first_sums(at_y, whole)
        sums, got = {}, {}
        for k, data[k], pieces[k], sums[k] in made:
            if k:
                got[k] = shift_y(sums[k], shifts[k])
        edge = halo(flags, pieces)
        total = (sums[0] + got[1]) + (got[2] + got[3])
        other = swap_z(total)
        edge = lax.optimization_barrier((edge, total))[0]
        base = smoothed(flags, pieces[0], pieces[3], pieces[1], edge, rows)
        mine = base - scale * (total + other)
    pieces = gathered(mine, shifts)
    return jnp.transpose(join(at_y, [pieces[k] for k in range(Y)], rows), (1, 0, 2))


def solution(mesh):
    days = P("tm", "space", None)
    fields = P(None, "space", None)
    return jax.shard_map(
        on_device,
        mesh=mesh,
        in_specs=(days, days, days, fields),
        out_specs=fields,
        check_vma=False,
    )
```

time: 131 us -> 98.9 us (0.75); the launches traced: 131 us -> 97 us
  waiting for transfers between devices: 74 us -> 47.8 us
  other arithmetic: 24.6 us -> 2.13 us
  Pallas kernels: 0 us -> 17.2 us
  local copies, waits for them, and re-layouts: 5.34 us -> 0.01 us
  starting transfers between devices: 26.7 us -> 29.5 us
    ppermute x14 -> x16, waiting for transfers between devices: 74 us -> 47.8 us  [the longest x12 33.7 us: shift_y(): lax.ppermute(block, 'tm', [(i, i // Y * Y + (i + by) % Y) for i in range(...]
    pallas_call x0 -> x9, Pallas kernels: none -> 17.2 us  [the longest x8 16.3 us: call(): pl.pallas_call(kernel, in_specs=in_specs, out_specs=[VMEM] * len(shapes),...]
    reduce_sum x4 -> x0, other arithmetic: 12.5 us -> none  [the longest x2 9.23 us: day_sums(): jnp.sum(dvar * base_exp, axis=0)]
    sub x8 -> x6, other arithmetic: 10.8 us -> 1.29 us  [the longest x4 0.78 us: laplace(): steps = middle[..., 1:] - middle[..., :-1]]
    slice x3 -> x0, local copies, waits for them, and re-layouts: 3.34 us -> none  [the longest x1 3.33 us: on_device(): theta[1]]
    ppermute x14 -> x16, starting transfers between devices: 26.7 us -> 29.5 us  [the longest x12 13.8 us: shift_y(): lax.ppermute(block, 'tm', [(i, i // Y * Y + (i + by) % Y) for i in range(...]
    another operation x1 -> x0, local copies, waits for them, and re-layouts: 1.52 us -> none  [on_device(): jnp.stack([jnp.where(first_low, pair[0], across[0]), jnp.where(first_low,...]
  transfers between devices with their start and end apart: 14 -> 16, of which waited for: 14 -> 10; matrix products, arithmetic and copies ran while one was open for 1% -> 2% of each run, Pallas kernels for 0% -> 8%
where the time goes in v2:
time: 98.9 us; the launch traced here: 97 us
  waiting for transfers between devices  47.8 us (48%)
  starting transfers between devices  29.5 us (30%)
  Pallas kernels  17.2 us (17%)
  other arithmetic  2.13 us (2%)
    ppermute x12, waiting for transfers between devices, shift_y(): lax.ppermute(block, 'tm', [(i, i // Y * Y + (i + by) % Y) for i in range(...  33.7 us
    pallas_call x8, Pallas kernels, call(): pl.pallas_call(kernel, in_specs=in_specs, out_specs=[VMEM] * len(shapes),...  16.3 us
    ppermute x2, waiting for transfers between devices, swap_z(): lax.ppermute(block, 'tm', [(i, i ^ Y) for i in range(lax.axis_size('tm'))])  14.1 us
    ppermute x12, starting transfers between devices, shift_y(): lax.ppermute(block, 'tm', [(i, i // Y * Y + (i + by) % Y) for i in range(...  13.8 us
    ppermute x2, starting transfers between devices, swap_z(): lax.ppermute(block, 'tm', [(i, i ^ Y) for i in range(lax.axis_size('tm'))])  11.8 us
    ppermute x2, starting transfers between devices, halo(): return lax.ppermute(send, ('tm', 'space'), pairs)  3.83 us
  transfers between devices with their start and end apart: 16, of which 10 were waited for; matrix products, arithmetic and copies ran while one was open for 2% of the time, Pallas kernels for 8%

profile of v2, /device:TPU:64, one launch (start us, length us, event | category | flops | bytes accessed | tf_op | source)
XLA Modules:
  0.0 97.0 jit_solution(5904504880537218174)
XLA Ops:
  0.0 4.2 %shard_map.55 = (f32[23,4,640]{2,1,0:T(4,128)S(1)}, f32[23,16,640]{2,1,0:T(8,128)S(1)}, f32[23,16,640]{2,1,0:T(8,128)S(1)}, f32[23,16,640]{2,1,0:T(8,128)S(1)}, ...) custom-call(s32[1]{0:T(128)} %bitcast.at_y, ...), custom_call_target="tpu_custom_call" | custom-call | flops 9420800 | bytes 2826240 | tf_op jit(solution)/shard_map/pallas_call | solution.py:178
  4.2 2.1 %shard_map.56 = (f32[23,4,640]{2,1,0:T(4,128)S(1)}, f32[23,16,640]{2,1,0:T(8,128)S(1)}, f32[23,16,640]{2,1,0:T(8,128)S(1)}, f32[23,16,640]{2,1,0:T(8,128)S(1)}, f32[23,4,640]{2,1,0:T(4,128)S(1)}) custom-call(s32[1]{0:T(128)} %bitcast.at_y, f32[90,16,640]{2,1,0:T(8,128)} %bitcast.7, f32[90,16,640]{2,1,0:T(8,128)} %bitcast.10, f32[90,16,640]{2,1,0:T(8,128)} %bitcast.13, ...), custom_call_target="tpu_custom_call" | custom-call | flops 9420800 | bytes 2826240 | tf_op jit(solution)/shard_map/pallas_call | solution.py:178
  6.3 2.1 %shard_map.57 = (f32[23,4,640]{2,1,0:T(4,128)S(1)}, f32[23,16,640]{2,1,0:T(8,128)S(1)}, f32[23,16,640]{2,1,0:T(8,128)S(1)}, f32[23,16,640]{2,1,0:T(8,128)S(1)}, f32[23,4,640]{2,1,0:T(4,128)S(1)}) custom-call(s32[1]{0:T(128)} %bitcast.at_y, f32[90,16,640]{2,1,0:T(8,128)} %bitcast.8, f32[90,16,640]{2,1,0:T(8,128)} %bitcast.11, f32[90,16,640]{2,1,0:T(8,128)} %bitcast.14, ...), custom_call_target="tpu_custom_call" | custom-call | flops 9420800 | bytes 2826240 | tf_op jit(solution)/shard_map/pallas_call | solution.py:178
  8.4 3.1 %collective-permute-start.3 = (f32[23,4,640]{2,1,0:T(4,128)S(1)}, f32[23,4,640]{2,1,0:T(4,128)S(1)}, u32[]{:S(2)}, u32[]{:S(2)}) collective-permute-start(f32[23,4,640]{2,1,0:T(4,128)S(1)} %get-tuple-element.46), channel_id=1, source_target_pairs={{0,96},{32,0},{64,32},{96,64},{128,224},{160,128},{192,160},{224,1... | collective-permute-start | bytes 706568 | tf_op jit(solution)/shard_map/ppermute | solution.py:246
  11.5 0.0 collective-permute-start.1
  11.5 2.2 %collective-permute-start.2 = (f32[23,4,640]{2,1,0:T(4,128)S(1)}, f32[23,4,640]{2,1,0:T(4,128)S(1)}, u32[]{:S(2)}, u32[]{:S(2)}) collective-permute-start(f32[23,4,640]{2,1,0:T(4,128)S(1)} %get-tuple-element.45), channel_id=1, source_target_pairs={{0,64},{32,96},{64,0},{96,32},{128,192},{160,224},{192,128},{224,1... | collective-permute-start | bytes 706568 | tf_op jit(solution)/shard_map/ppermute | solution.py:246
  13.7 1.9 %collective-permute-start = (f32[2,4,640]{2,1,0:T(4,128)S(1)}, f32[2,4,640]{2,1,0:T(4,128)S(1)}, u32[]{:S(2)}, u32[]{:S(2)}) collective-permute-start(f32[2,4,640]{2,1,0:T(4,128)S(1)} %slice_select_fusion.3), channel_id=1, source_target_pairs={{0,1},{97,96},{1,2},{98,97},{2,3},{99,98},{3,4},{100,99},{4,5},{10... | collective-permute-start | bytes 61448 | tf_op jit(solution)/shard_map/ppermute | solution.py:262
  15.6 0.0 copy-start
  15.7 1.6 %shard_map.58 = f32[23,4,640]{2,1,0:T(4,128)S(1)} custom-call(f32[23,4,640]{2,1,0:T(4,128)S(1)} %get-tuple-element.38.refs_0_, f32[23,16,640]{2,1,0:T(8,128)S(1)} %get-tuple-element.41.refs_1_, f32[23,16,640]{2,1,0:T(8,128)S(1)} %get-tuple-element.42.refs_2_, f32[23,16,640]{2,1,0:T(8,128)S(1)} %get-tuple-element.43.refs_3_), custom_call_target="tpu_custom_call" | custom-call | flops 9420800 | bytes 2826240 | tf_op jit(solution)/shard_map/pallas_call | solution.py:178
  17.2 4.3 %collective-permute-done.3 = f32[23,4,640]{2,1,0:T(4,128)S(1)} collective-permute-done((f32[23,4,640]{2,1,0:T(4,128)S(1)}, f32[23,4,640]{2,1,0:T(4,128)S(1)}, u32[]{:S(2)}, u32[]{:S(2)}) %collective-permute-start.3) | collective-permute-done | bytes 235552 | tf_op jit(solution)/shard_map/ppermute | solution.py:246
  21.6 3.4 %collective-permute-done.1 = f32[23,4,640]{2,1,0:T(4,128)S(1)} collective-permute-done((f32[23,4,640]{2,1,0:T(4,128)S(1)}, f32[23,4,640]{2,1,0:T(4,128)S(1)}, u32[]{:S(2)}, u32[]{:S(2)}) %collective-permute-start.1) | collective-permute-done | bytes 235552 | tf_op jit(solution)/shard_map/ppermute | solution.py:246
  25.0 0.0 collective-permute-done.2
  25.0 0.1 add_add_fusion.1
  25.1 5.5 %collective-permute-start.4 = (f32[23,4,640]{2,1,0:T(4,128)S(1)}, f32[23,4,640]{2,1,0:T(4,128)S(1)}, u32[]{:S(2)}, u32[]{:S(2)}) collective-permute-start(f32[23,4,640]{2,1,0:T(4,128)S(1)} %add_add_fusion.1), channel_id=1, source_target_pairs={{0,128},{32,160},{64,192},{96,224},{128,0},{160,32},{192,64},{224,... | collective-permute-start | bytes 706568 | tf_op jit(solution)/shard_map/ppermute | solution.py:250
  30.6 0.0 collective-permute-done
  30.6 0.1 pad_maximum_fusion
  30.7 0.2 slice_subtract_fusion.1
  30.9 0.2 fusion.3
  31.1 0.2 slice_subtract_fusion.3
  31.3 8.3 %collective-permute-done.4 = f32[23,4,640]{2,1,0:T(4,128)S(1)} collective-permute-done((f32[23,4,640]{2,1,0:T(4,128)S(1)}, f32[23,4,640]{2,1,0:T(4,128)S(1)}, u32[]{:S(2)}, u32[]{:S(2)}) %collective-permute-start.4) | collective-permute-done | bytes 235552 | tf_op jit(solution)/shard_map/ppermute | solution.py:250
  39.6 0.0 copy-done
  39.6 0.3 fusion.13.refs_0_
  39.8 1.7 %collective-permute-start.6 = (f32[23,4,640]{2,1,0:T(4,128)S(1)}, f32[23,4,640]{2,1,0:T(4,128)S(1)}, u32[]{:S(2)}, u32[]{:S(2)}) collective-permute-start(f32[23,4,640]{2,1,0:T(4,128)S(1)} %fusion.13.refs_0_), channel_id=1, source_target_pairs={{0,96},{32,0},{64,32},{96,64},{128,224},{160,128},{192,160},{224,1... | collective-permute-start | bytes 706568 | tf_op jit(solution)/shard_map/ppermute | solution.py:246
  41.5 0.4 collective-permute-start.5
  42.0 1.9 %collective-permute-start.9 = (f32[23,4,640]{2,1,0:T(4,128)S(1)}, f32[23,4,640]{2,1,0:T(4,128)S(1)}, u32[]{:S(2)}, u32[]{:S(2)}) collective-permute-start(f32[23,4,640]{2,1,0:T(4,128)S(1)} %fusion.13.refs_0_), channel_id=1, source_target_pairs={{0,64},{32,96},{64,0},{96,32},{128,192},{160,224},{192,128},{224,1... | collective-permute-start | bytes 706568 | tf_op jit(solution)/shard_map/ppermute | solution.py:246
  43.8 4.7 %collective-permute-done.6.refs_0_ = f32[23,4,640]{2,1,0:T(4,128)S(1)} collective-permute-done((f32[23,4,640]{2,1,0:T(4,128)S(1)}, f32[23,4,640]{2,1,0:T(4,128)S(1)}, u32[]{:S(2)}, u32[]{:S(2)}) %collective-permute-start.6) | collective-permute-done | bytes 235552 | tf_op jit(solution)/shard_map/ppermute | solution.py:246
  48.5 1.6 %shard_map.60 = f32[23,4,640]{2,1,0:T(4,128)S(1)} custom-call(f32[23,4,640]{2,1,0:T(4,128)S(1)} %collective-permute-done.6.refs_0_, f32[23,16,640]{2,1,0:T(8,128)S(1)} %get-tuple-element.30.refs_4_.refs_1_, f32[23,16,640]{2,1,0:T(8,128)S(1)} %get-tuple-element.31.refs_5_.refs_2_, f32[23,16,640]{2,1,0:T(8,128)S(1)} %get-tuple-element.32.refs_6_.refs_3_), custom_call_target="tpu_custom_call" | custom-call | flops 9420800 | bytes 2826240 | tf_op jit(solution)/shard_map/pallas_call | solution.py:178
  50.1 0.1 collective-permute-start.8
  50.2 4.9 %collective-permute-done.5.refs_0_ = f32[23,4,640]{2,1,0:T(4,128)S(1)} collective-permute-done((f32[23,4,640]{2,1,0:T(4,128)S(1)}, f32[23,4,640]{2,1,0:T(4,128)S(1)}, u32[]{:S(2)}, u32[]{:S(2)}) %collective-permute-start.5) | collective-permute-done | bytes 235552 | tf_op jit(solution)/shard_map/ppermute | solution.py:246
  55.1 1.6 %shard_map.62 = f32[23,4,640]{2,1,0:T(4,128)S(1)} custom-call(f32[23,4,640]{2,1,0:T(4,128)S(1)} %collective-permute-done.5.refs_0_, f32[23,16,640]{2,1,0:T(8,128)S(1)} %get-tuple-element.34.refs_4_.refs_1_, f32[23,16,640]{2,1,0:T(8,128)S(1)} %get-tuple-element.35.refs_5_.refs_2_, f32[23,16,640]{2,1,0:T(8,128)S(1)} %get-tuple-element.36.refs_6_.refs_3_), custom_call_target="tpu_custom_call" | custom-call | flops 9420800 | bytes 2826240 | tf_op jit(solution)/shard_map/pallas_call | solution.py:178
  56.7 0.1 collective-permute-start.11
  56.8 0.0 collective-permute-done.9.refs_0_
  56.8 1.6 %shard_map.61 = f32[23,4,640]{2,1,0:T(4,128)S(1)} custom-call(f32[23,4,640]{2,1,0:T(4,128)S(1)} %collective-permute-done.9.refs_0_, f32[23,16,640]{2,1,0:T(8,128)S(1)} %get-tuple-element.49.refs_1_, f32[23,16,640]{2,1,0:T(8,128)S(1)} %get-tuple-element.50.refs_2_, f32[23,16,640]{2,1,0:T(8,128)S(1)} %get-tuple-element.51.refs_3_), custom_call_target="tpu_custom_call" | custom-call | flops 9420800 | bytes 2826240 | tf_op jit(solution)/shard_map/pallas_call | solution.py:178
  58.4 0.6 collective-permute-start.10
  59.0 1.6 %shard_map.59 = f32[23,4,640]{2,1,0:T(4,128)S(1)} custom-call(f32[23,4,640]{2,1,0:T(4,128)S(1)} %fusion.13.refs_0_, f32[23,16,640]{2,1,0:T(8,128)S(1)} %get-tuple-element.41.refs_1_, f32[23,16,640]{2,1,0:T(8,128)S(1)} %get-tuple-element.42.refs_2_, f32[23,16,640]{2,1,0:T(8,128)S(1)} %get-tuple-element.43.refs_3_), custom_call_target="tpu_custom_call" | custom-call | flops 9420800 | bytes 2826240 | tf_op jit(solution)/shard_map/pallas_call | solution.py:178
  60.6 1.9 %collective-permute-start.7 = (f32[2,4,640]{2,1,0:T(4,128)S(1)}, f32[2,4,640]{2,1,0:T(4,128)S(1)}, u32[]{:S(2)}, u32[]{:S(2)}) collective-permute-start(f32[2,4,640]{2,1,0:T(4,128)S(1)} %slice_select_fusion.2), channel_id=1, source_target_pairs={{0,1},{97,96},{1,2},{98,97},{2,3},{99,98},{3,4},{100,99},{4,5},{10... | collective-permute-start | bytes 61448 | tf_op jit(solution)/shard_map/ppermute | solution.py:262
  62.5 0.0 collective-permute-done.8
  62.5 0.3 collective-permute-done.11
  62.8 3.4 %collective-permute-done.10 = f32[23,4,640]{2,1,0:T(4,128)S(1)} collective-permute-done((f32[23,4,640]{2,1,0:T(4,128)S(1)}, f32[23,4,640]{2,1,0:T(4,128)S(1)}, u32[]{:S(2)}, u32[]{:S(2)}) %collective-permute-start.10) | collective-permute-done | bytes 235552 | tf_op jit(solution)/shard_map/ppermute | solution.py:246
  66.2 0.1 add_add_fusion
  66.3 6.4 %collective-permute-start.12 = (f32[23,4,640]{2,1,0:T(4,128)S(1)}, f32[23,4,640]{2,1,0:T(4,128)S(1)}, u32[]{:S(2)}, u32[]{:S(2)}) collective-permute-start(f32[23,4,640]{2,1,0:T(4,128)S(1)} %add_add_fusion), channel_id=1, source_target_pairs={{0,128},{32,160},{64,192},{96,224},{128,0},{160,32},{192,64},{224,... | collective-permute-start | bytes 706568 | tf_op jit(solution)/shard_map/ppermute | solution.py:250
  72.7 0.0 collective-permute-done.7
  72.7 0.1 pad_maximum_fusion.1
  72.8 0.2 slice_subtract_fusion
  73.0 0.2 fusion.1
  73.2 0.2 slice_subtract_fusion.2
  73.4 5.8 %collective-permute-done.12 = f32[23,4,640]{2,1,0:T(4,128)S(1)} collective-permute-done((f32[23,4,640]{2,1,0:T(4,128)S(1)}, f32[23,4,640]{2,1,0:T(4,128)S(1)}, u32[]{:S(2)}, u32[]{:S(2)}) %collective-permute-start.12) | collective-permute-done | bytes 235552 | tf_op jit(solution)/shard_map/ppermute | solution.py:250
  79.2 0.3 fusion.8.refs_0_
  79.5 2.8 %collective-permute-start.13 = (f32[23,4,640]{2,1,0:T(4,128)S(1)}, f32[23,4,640]{2,1,0:T(4,128)S(1)}, u32[]{:S(2)}, u32[]{:S(2)}) collective-permute-start(f32[23,4,640]{2,1,0:T(4,128)S(1)} %fusion.8.refs_0_), channel_id=1, source_target_pairs={{0,96},{32,0},{64,32},{96,64},{128,224},{160,128},{192,160},{224,1... | collective-permute-start | bytes 706568 | tf_op jit(solution)/shard_map/ppermute | solution.py:246
  82.2 0.0 collective-permute-start.14
  82.2 1.0 collective-permute-start.15
  83.2 9.3 %collective-permute-done.13.refs_1_ = f32[23,4,640]{2,1,0:T(4,128)S(1)} collective-permute-done((f32[23,4,640]{2,1,0:T(4,128)S(1)}, f32[23,4,640]{2,1,0:T(4,128)S(1)}, u32[]{:S(2)}, u32[]{:S(2)}) %collective-permute-start.13) | collective-permute-done | bytes 235552 | tf_op jit(solution)/shard_map/ppermute | solution.py:246
  92.5 0.0 collective-permute-done.14.refs_2_
  92.5 3.4 %collective-permute-done.15.refs_3_ = f32[23,4,640]{2,1,0:T(4,128)S(1)} collective-permute-done((f32[23,4,640]{2,1,0:T(4,128)S(1)}, f32[23,4,640]{2,1,0:T(4,128)S(1)}, u32[]{:S(2)}, u32[]{:S(2)}) %collective-permute-start.15) | collective-permute-done | bytes 235552 | tf_op jit(solution)/shard_map/ppermute | solution.py:246
  95.9 0.9 join.1
  (4 shorter events, 0.1 us)
Async XLA Ops:
  8.4 13.1 %collective-permute-start.3 = (f32[23,4,640]{2,1,0:T(4,128)S(1)}, f32[23,4,640]{2,1,0:T(4,128)S(1)}, u32[]{:S(2)}, u32[]{:S(2)}) collective-permute-start(f32[23,4,640]{2,1,0:T(4,128)S(1)} %get-tuple-element.46), channel_id=1, source_target_pairs={{0,96},{32,0},{64,32},{96,64},{128,224},{160,128},{192,160},{224,1... | collective-permute-start | bytes 706568 | tf_op jit(solution)/shard_map/ppermute | solution.py:246
  11.5 13.5 %collective-permute-start.1 = (f32[23,4,640]{2,1,0:T(4,128)S(1)}, f32[23,4,640]{2,1,0:T(4,128)S(1)}, u32[]{:S(2)}, u32[]{:S(2)}) collective-permute-start(f32[23,4,640]{2,1,0:T(4,128)S(1)} %get-tuple-element.44), channel_id=1, source_target_pairs={{0,32},{32,64},{64,96},{96,0},{128,160},{160,192},{192,224},{224,1... | collective-permute-start | bytes 706568 | tf_op jit(solution)/shard_map/ppermute | solution.py:246
  11.5 13.5 %collective-permute-start.2 = (f32[23,4,640]{2,1,0:T(4,128)S(1)}, f32[23,4,640]{2,1,0:T(4,128)S(1)}, u32[]{:S(2)}, u32[]{:S(2)}) collective-permute-start(f32[23,4,640]{2,1,0:T(4,128)S(1)} %get-tuple-element.45), channel_id=1, source_target_pairs={{0,64},{32,96},{64,0},{96,32},{128,192},{160,224},{192,128},{224,1... | collective-permute-start | bytes 706568 | tf_op jit(solution)/shard_map/ppermute | solution.py:246
  13.7 16.8 %collective-permute-start = (f32[2,4,640]{2,1,0:T(4,128)S(1)}, f32[2,4,640]{2,1,0:T(4,128)S(1)}, u32[]{:S(2)}, u32[]{:S(2)}) collective-permute-start(f32[2,4,640]{2,1,0:T(4,128)S(1)} %slice_select_fusion.3), channel_id=1, source_target_pairs={{0,1},{97,96},{1,2},{98,97},{2,3},{99,98},{3,4},{100,99},{4,5},{10... | collective-permute-start | bytes 61448 | tf_op jit(solution)/shard_map/ppermute | solution.py:262
  15.6 23.9 %copy-start = (f32[4]{0:T(128)S(1)}, f32[4]{0:T(128)}, u32[]{:S(2)}) copy-start(f32[4]{0:T(128)} %constant.56) | copy-start | bytes 52
  25.1 14.5 %collective-permute-start.4 = (f32[23,4,640]{2,1,0:T(4,128)S(1)}, f32[23,4,640]{2,1,0:T(4,128)S(1)}, u32[]{:S(2)}, u32[]{:S(2)}) collective-permute-start(f32[23,4,640]{2,1,0:T(4,128)S(1)} %add_add_fusion.1), channel_id=1, source_target_pairs={{0,128},{32,160},{64,192},{96,224},{128,0},{160,32},{192,64},{224,... | collective-permute-start | bytes 706568 | tf_op jit(solution)/shard_map/ppermute | solution.py:250
  39.8 8.7 %collective-permute-start.6 = (f32[23,4,640]{2,1,0:T(4,128)S(1)}, f32[23,4,640]{2,1,0:T(4,128)S(1)}, u32[]{:S(2)}, u32[]{:S(2)}) collective-permute-start(f32[23,4,640]{2,1,0:T(4,128)S(1)} %fusion.13.refs_0_), channel_id=1, source_target_pairs={{0,96},{32,0},{64,32},{96,64},{128,224},{160,128},{192,160},{224,1... | collective-permute-start | bytes 706568 | tf_op jit(solution)/shard_map/ppermute | solution.py:246
  41.5 13.6 %collective-permute-start.5 = (f32[23,4,640]{2,1,0:T(4,128)S(1)}, f32[23,4,640]{2,1,0:T(4,128)S(1)}, u32[]{:S(2)}, u32[]{:S(2)}) collective-permute-start(f32[23,4,640]{2,1,0:T(4,128)S(1)} %fusion.13.refs_0_), channel_id=1, source_target_pairs={{0,32},{32,64},{64,96},{96,0},{128,160},{160,192},{192,224},{224,1... | collective-permute-start | bytes 706568 | tf_op jit(solution)/shard_map/ppermute | solution.py:246
  42.0 14.8 %collective-permute-start.9 = (f32[23,4,640]{2,1,0:T(4,128)S(1)}, f32[23,4,640]{2,1,0:T(4,128)S(1)}, u32[]{:S(2)}, u32[]{:S(2)}) collective-permute-start(f32[23,4,640]{2,1,0:T(4,128)S(1)} %fusion.13.refs_0_), channel_id=1, source_target_pairs={{0,64},{32,96},{64,0},{96,32},{128,192},{160,224},{192,128},{224,1... | collective-permute-start | bytes 706568 | tf_op jit(solution)/shard_map/ppermute | solution.py:246
  50.1 12.4 %collective-permute-start.8 = (f32[23,4,640]{2,1,0:T(4,128)S(1)}, f32[23,4,640]{2,1,0:T(4,128)S(1)}, u32[]{:S(2)}, u32[]{:S(2)}) collective-permute-start(f32[23,4,640]{2,1,0:T(4,128)S(1)} %shard_map.60), channel_id=1, source_target_pairs={{0,32},{32,64},{64,96},{96,0},{128,160},{160,192},{192,224},{224,1... | collective-permute-start | bytes 706568 | tf_op jit(solution)/shard_map/ppermute | solution.py:246
  56.7 6.2 %collective-permute-start.11 = (f32[23,4,640]{2,1,0:T(4,128)S(1)}, f32[23,4,640]{2,1,0:T(4,128)S(1)}, u32[]{:S(2)}, u32[]{:S(2)}) collective-permute-start(f32[23,4,640]{2,1,0:T(4,128)S(1)} %shard_map.62), channel_id=1, source_target_pairs={{0,96},{32,0},{64,32},{96,64},{128,224},{160,128},{192,160},{224,1... | collective-permute-start | bytes 706568 | tf_op jit(solution)/shard_map/ppermute | solution.py:246
  58.4 7.9 %collective-permute-start.10 = (f32[23,4,640]{2,1,0:T(4,128)S(1)}, f32[23,4,640]{2,1,0:T(4,128)S(1)}, u32[]{:S(2)}, u32[]{:S(2)}) collective-permute-start(f32[23,4,640]{2,1,0:T(4,128)S(1)} %shard_map.61), channel_id=1, source_target_pairs={{0,64},{32,96},{64,0},{96,32},{128,192},{160,224},{192,128},{224,1... | collective-permute-start | bytes 706568 | tf_op jit(solution)/shard_map/ppermute | solution.py:246
  60.6 12.1 %collective-permute-start.7 = (f32[2,4,640]{2,1,0:T(4,128)S(1)}, f32[2,4,640]{2,1,0:T(4,128)S(1)}, u32[]{:S(2)}, u32[]{:S(2)}) collective-permute-start(f32[2,4,640]{2,1,0:T(4,128)S(1)} %slice_select_fusion.2), channel_id=1, source_target_pairs={{0,1},{97,96},{1,2},{98,97},{2,3},{99,98},{3,4},{100,99},{4,5},{10... | collective-permute-start | bytes 61448 | tf_op jit(solution)/shard_map/ppermute | solution.py:262
  66.3 12.9 %collective-permute-start.12 = (f32[23,4,640]{2,1,0:T(4,128)S(1)}, f32[23,4,640]{2,1,0:T(4,128)S(1)}, u32[]{:S(2)}, u32[]{:S(2)}) collective-permute-start(f32[23,4,640]{2,1,0:T(4,128)S(1)} %add_add_fusion), channel_id=1, source_target_pairs={{0,128},{32,160},{64,192},{96,224},{128,0},{160,32},{192,64},{224,... | collective-permute-start | bytes 706568 | tf_op jit(solution)/shard_map/ppermute | solution.py:250
  79.5 13.0 %collective-permute-start.13 = (f32[23,4,640]{2,1,0:T(4,128)S(1)}, f32[23,4,640]{2,1,0:T(4,128)S(1)}, u32[]{:S(2)}, u32[]{:S(2)}) collective-permute-start(f32[23,4,640]{2,1,0:T(4,128)S(1)} %fusion.8.refs_0_), channel_id=1, source_target_pairs={{0,96},{32,0},{64,32},{96,64},{128,224},{160,128},{192,160},{224,1... | collective-permute-start | bytes 706568 | tf_op jit(solution)/shard_map/ppermute | solution.py:246
  82.2 10.3 %collective-permute-start.14 = (f32[23,4,640]{2,1,0:T(4,128)S(1)}, f32[23,4,640]{2,1,0:T(4,128)S(1)}, u32[]{:S(2)}, u32[]{:S(2)}) collective-permute-start(f32[23,4,640]{2,1,0:T(4,128)S(1)} %fusion.8.refs_0_), channel_id=1, source_target_pairs={{0,64},{32,96},{64,0},{96,32},{128,192},{160,224},{192,128},{224,1... | collective-permute-start | bytes 706568 | tf_op jit(solution)/shard_map/ppermute | solution.py:246
  82.2 13.6 %collective-permute-start.15 = (f32[23,4,640]{2,1,0:T(4,128)S(1)}, f32[23,4,640]{2,1,0:T(4,128)S(1)}, u32[]{:S(2)}, u32[]{:S(2)}) collective-permute-start(f32[23,4,640]{2,1,0:T(4,128)S(1)} %fusion.8.refs_0_), channel_id=1, source_target_pairs={{0,32},{32,64},{64,96},{96,0},{128,160},{160,192},{192,224},{224,1... | collective-permute-start | bytes 706568 | tf_op jit(solution)/shard_map/ppermute | solution.py:246

commit v3 on v2

--- a/solution.py
+++ b/solution.py
@@ -91,7 +91,7 @@
 
 def quarter_copies(at_y, k, sources, targets, sems):
     rows, tall = sources[0].shape[0], targets[0].shape[0]
-    first = first_of((at_y[0] + k) % Y, rows)
+    first = first_of(at_y[0] ^ k, rows)
 
     def group(start, size, i):
         return [
@@ -146,7 +146,7 @@
     shorter = rows - (Y - 1) * tall
     for go in (True, False):
         for k in range(Y):
-            which = (at_y[0] + k) % Y
+            which = at_y[0] ^ k
 
             @pl.when(which != Y - 2)
             def _(k=k, which=which):
@@ -213,10 +213,10 @@
     yield ORDER[3], ahead[:3], ahead[3], later_sums(ahead[:3], ahead[3])
 
 
-def gathered(mine, shifts):
+def gathered(mine):
     pieces = {0: mine}
     for k in (2, 1, 3):
-        pieces[k] = shift_y(mine, -shifts[k])
+        pieces[k] = swap_y(mine, k)
     return pieces
 
 
@@ -241,24 +241,21 @@
     )(at_y, *pieces)
 
 
-def shift_y(block, by):
-    count = lax.axis_size("tm")
-    return lax.ppermute(block, "tm", [(i, i // Y * Y + (i + by) % Y) for i in range(count)])
+def swap_y(block, k):
+    return lax.ppermute(block, "tm", [(i, i ^ k) for i in range(lax.axis_size("tm"))])
 
 
 def swap_z(block):
     return lax.ppermute(block, "tm", [(i, i ^ Y) for i in range(lax.axis_size("tm"))])
 
 
-def halo(flags, pieces):
-    send = jnp.where(flags["first"], pieces[3][-2:], pieces[1][:2])
-    groups, count = lax.axis_size("tm") // Y, lax.axis_size("space")
+def halo(flags, across):
+    send = jnp.where(flags["first"], across[-2:], across[:2])
+    count = lax.axis_size("space")
     pairs = []
-    for g in range(groups):
-        for s in range(count):
-            over = (g + s // (count - 1)) % groups
-            pairs.append(((g * Y) * count + s, over * Y * count + (s + 1) % count))
-            pairs.append((((over + 1) * Y - 1) * count + (s + 1) % count, ((g + 1) * Y - 1) * count + s))
+    for t in range(lax.axis_size("tm")):
+        by = 1 if t % Y < Y // 2 else -1
+        pairs += [(t * count + s, t * count + (s + by) % count) for s in range(count)]
     return lax.ppermute(send, ("tm", "space"), pairs)
 
 
@@ -272,12 +269,14 @@
     )
 
 
-def smoothed(flags, mine, below, above, edge, rows):
-    shared = Y * mine.shape[0] - rows
+def smoothed(flags, mine, near, far, edge, rows):
     tall = mine.shape[0]
-    low = jnp.where(flags["last"], below[tall - shared - 2 : tall - shared], below[-2:])
+    shared = Y * tall - rows
+    low = jnp.where(flags["odd"], near[-2:], far[-2:])
+    low = jnp.where(flags["last"], near[tall - shared - 2 : tall - shared], low)
     low = jnp.where(flags["first"], edge, low)
-    high = jnp.where(flags["third"], above[shared : shared + 2], above[:2])
+    high = jnp.where(flags["odd"], far[:2], near[:2])
+    high = jnp.where(flags["third"], near[shared : shared + 2], high)
     high = jnp.where(flags["last"], edge, high)
     return mine - (STEP * SMOOTH) * laplace(laplace(jnp.concatenate([low, mine, high])))
 
@@ -287,28 +286,31 @@
     scale = jnp.array(FACTORS, jnp.float32).reshape(1, 4, 1) * (STEP / (days * lax.axis_size("tm")))
     y = lax.axis_index("tm") % Y
     at_y = jnp.reshape(y, (1,)).astype(jnp.int32)
-    flags = {"first": y == 0, "third": y == Y - 2, "last": y == Y - 1}
+    flags = {"first": y == 0, "odd": y % 2 == 1, "third": y == Y - 2, "last": y == Y - 1}
     at_y, flags = lax.optimization_barrier((at_y, flags))
     whole = [jnp.transpose(x, (1, 0, 2)) for x in (fmean, fvar, obs, theta)]
-    shifts = {1: 1, 2: 2, 3: -1}
     data, pieces = {}, {}
     for step in range(ITERS):
         if step:
-            pieces = gathered(mine, shifts)
+            pieces = gathered(mine)
             made = later_steps(data, pieces)
         else:
             made = first_sums(at_y, whole)
         sums, got = {}, {}
         for k, data[k], pieces[k], sums[k] in made:
-            if k:
-                got[k] = shift_y(sums[k], shifts[k])
-        edge = halo(flags, pieces)
-        total = (sums[0] + got[1]) + (got[2] + got[3])
+            if k == 2:
+                relayed = swap_y(sums[2], 1)
+            elif k == 1:
+                got[1] = swap_y(sums[1], 1)
+            elif k == 3:
+                got[3] = swap_y(sums[3] + relayed, 3)
+        edge = halo(flags, pieces[3])
+        total = (sums[0] + got[1]) + got[3]
         other = swap_z(total)
         edge = lax.optimization_barrier((edge, total))[0]
-        base = smoothed(flags, pieces[0], pieces[3], pieces[1], edge, rows)
+        base = smoothed(flags, pieces[0], pieces[1], pieces[3], edge, rows)
         mine = base - scale * (total + other)
-    pieces = gathered(mine, shifts)
+    pieces = gathered(mine)
     return jnp.transpose(join(at_y, [pieces[k] for k in range(Y)], rows), (1, 0, 2))
 
 

time: 98.9 us -> 93.8 us (0.948)
  waiting for transfers between devices: 47.8 us -> 43.5 us
    ppermute x12, waiting for transfers between devices: 33.7 us -> 25.9 us  [swap_y(): lax.ppermute(block, 'tm', [(i, i ^ k) for i in range(lax.axis_size('tm'))])]
    ppermute x12, starting transfers between devices: 13.8 us -> 18.4 us  [swap_y(): lax.ppermute(block, 'tm', [(i, i ^ k) for i in range(lax.axis_size('tm'))])]
    ppermute x2, starting transfers between devices: 3.83 us -> 0.27 us  [halo(): return lax.ppermute(send, ('tm', 'space'), pairs)]
    ppermute x2, waiting for transfers between devices: 14.1 us -> 17.6 us  [swap_z(): lax.ppermute(block, 'tm', [(i, i ^ Y) for i in range(lax.axis_size('tm'))])]
    ppermute x2, starting transfers between devices: 11.8 us -> 10.5 us  [swap_z(): lax.ppermute(block, 'tm', [(i, i ^ Y) for i in range(lax.axis_size('tm'))])]
  transfers between devices with their start and end apart: 16 -> 16, of which waited for: 10 -> 9; matrix products, arithmetic and copies ran while one was open for 2% -> 2% of each run, Pallas kernels for 8% -> 13%
where the time goes in v3:
time: 93.8 us; the launch traced here: 92.4 us
  waiting for transfers between devices  43.5 us (46%)
  starting transfers between devices  29.1 us (31%)
  Pallas kernels  17.2 us (18%)
  other arithmetic  2.22 us (2%)
    ppermute x12, waiting for transfers between devices, swap_y(): lax.ppermute(block, 'tm', [(i, i ^ k) for i in range(lax.axis_size('tm'))])  25.9 us
    ppermute x12, starting transfers between devices, swap_y(): lax.ppermute(block, 'tm', [(i, i ^ k) for i in range(lax.axis_size('tm'))])  18.4 us
    ppermute x2, waiting for transfers between devices, swap_z(): lax.ppermute(block, 'tm', [(i, i ^ Y) for i in range(lax.axis_size('tm'))])  17.6 us
    pallas_call x8, Pallas kernels, call(): pl.pallas_call(kernel, in_specs=in_specs, out_specs=[VMEM] * len(shapes),...  16.2 us
    ppermute x2, starting transfers between devices, swap_z(): lax.ppermute(block, 'tm', [(i, i ^ Y) for i in range(lax.axis_size('tm'))])  10.5 us
  transfers between devices with their start and end apart: 16, of which 9 were waited for; matrix products, arithmetic and copies ran while one was open for 2% of the time, Pallas kernels for 13%

profile of v3, /device:TPU:64, one launch (start us, length us, event | category | flops | bytes accessed | tf_op | source)
XLA Modules:
  0.0 92.4 jit_solution(6585367975137318798)
XLA Ops:
  0.0 4.2 %shard_map.55 = (f32[23,4,640]{2,1,0:T(4,128)S(1)}, f32[23,16,640]{2,1,0:T(8,128)S(1)}, f32[23,16,640]{2,1,0:T(8,128)S(1)}, f32[23,16,640]{2,1,0:T(8,128)S(1)}, ...) custom-call(s32[1]{0:T(128)} %bitcast.at_y, ...), custom_call_target="tpu_custom_call" | custom-call | flops 9420800 | bytes 2826240 | tf_op jit(solution)/shard_map/pallas_call | solution.py:178
  4.2 1.7 %collective-permute-start.2 = (f32[23,4,640]{2,1,0:T(4,128)S(1)}, f32[23,4,640]{2,1,0:T(4,128)S(1)}, u32[]{:S(2)}, u32[]{:S(2)}) collective-permute-start(f32[23,4,640]{2,1,0:T(4,128)S(1)} %get-tuple-element.47), channel_id=1, source_target_pairs={{0,32},{32,0},{64,96},{96,64},{128,160},{160,128},{192,224},{224,1... | collective-permute-start | bytes 706568 | tf_op jit(solution)/shard_map/ppermute | solution.py:245
  5.8 2.1 %shard_map.56 = (f32[23,4,640]{2,1,0:T(4,128)S(1)}, f32[23,16,640]{2,1,0:T(8,128)S(1)}, f32[23,16,640]{2,1,0:T(8,128)S(1)}, f32[23,16,640]{2,1,0:T(8,128)S(1)}, f32[23,4,640]{2,1,0:T(4,128)S(1)}) custom-call(s32[1]{0:T(128)} %bitcast.at_y, f32[90,16,640]{2,1,0:T(8,128)} %bitcast.7, f32[90,16,640]{2,1,0:T(8,128)} %bitcast.10, f32[90,16,640]{2,1,0:T(8,128)} %bitcast.13, ...), custom_call_target="tpu_custom_call" | custom-call | flops 9420800 | bytes 2826240 | tf_op jit(solution)/shard_map/pallas_call | solution.py:178
  8.0 0.5 collective-permute-start.1
  8.5 2.1 %shard_map.57 = (f32[23,4,640]{2,1,0:T(4,128)S(1)}, f32[23,16,640]{2,1,0:T(8,128)S(1)}, f32[23,16,640]{2,1,0:T(8,128)S(1)}, f32[23,16,640]{2,1,0:T(8,128)S(1)}, f32[23,4,640]{2,1,0:T(4,128)S(1)}) custom-call(s32[1]{0:T(128)} %bitcast.at_y, f32[90,16,640]{2,1,0:T(8,128)} %bitcast.8, f32[90,16,640]{2,1,0:T(8,128)} %bitcast.11, f32[90,16,640]{2,1,0:T(8,128)} %bitcast.14, ...), custom_call_target="tpu_custom_call" | custom-call | flops 9420800 | bytes 2826240 | tf_op jit(solution)/shard_map/pallas_call | solution.py:178
  10.6 2.3 %collective-permute-done.2 = f32[23,4,640]{2,1,0:T(4,128)S(1)} collective-permute-done((f32[23,4,640]{2,1,0:T(4,128)S(1)}, f32[23,4,640]{2,1,0:T(4,128)S(1)}, u32[]{:S(2)}, u32[]{:S(2)}) %collective-permute-start.2) | collective-permute-done | bytes 235552 | tf_op jit(solution)/shard_map/ppermute | solution.py:245
  12.9 0.1 add.74
  12.9 3.1 %collective-permute-start.3 = (f32[23,4,640]{2,1,0:T(4,128)S(1)}, f32[23,4,640]{2,1,0:T(4,128)S(1)}, u32[]{:S(2)}, u32[]{:S(2)}) collective-permute-start(f32[23,4,640]{2,1,0:T(4,128)S(1)} %add.74), channel_id=1, source_target_pairs={{0,96},{32,64},{64,32},{96,0},{128,224},{160,192},{192,160},{224,1... | collective-permute-start | bytes 706568 | tf_op jit(solution)/shard_map/ppermute | solution.py:245
  16.1 0.0 collective-permute-start
  16.1 0.0 copy-start
  16.1 1.6 %shard_map.58 = f32[23,4,640]{2,1,0:T(4,128)S(1)} custom-call(f32[23,4,640]{2,1,0:T(4,128)S(1)} %get-tuple-element.39.refs_0_, f32[23,16,640]{2,1,0:T(8,128)S(1)} %get-tuple-element.42.refs_1_, f32[23,16,640]{2,1,0:T(8,128)S(1)} %get-tuple-element.43.refs_2_, f32[23,16,640]{2,1,0:T(8,128)S(1)} %get-tuple-element.44.refs_3_), custom_call_target="tpu_custom_call" | custom-call | flops 9420800 | bytes 2826240 | tf_op jit(solution)/shard_map/pallas_call | solution.py:178
  17.7 0.0 collective-permute-done.1
  17.7 2.7 %collective-permute-done.3 = f32[23,4,640]{2,1,0:T(4,128)S(1)} collective-permute-done((f32[23,4,640]{2,1,0:T(4,128)S(1)}, f32[23,4,640]{2,1,0:T(4,128)S(1)}, u32[]{:S(2)}, u32[]{:S(2)}) %collective-permute-start.3) | collective-permute-done | bytes 235552 | tf_op jit(solution)/shard_map/ppermute | solution.py:245
  20.3 0.1 add_add_fusion.1
  20.4 5.5 %collective-permute-start.4 = (f32[23,4,640]{2,1,0:T(4,128)S(1)}, f32[23,4,640]{2,1,0:T(4,128)S(1)}, u32[]{:S(2)}, u32[]{:S(2)}) collective-permute-start(f32[23,4,640]{2,1,0:T(4,128)S(1)} %add_add_fusion.1), channel_id=1, source_target_pairs={{0,128},{32,160},{64,192},{96,224},{128,0},{160,32},{192,64},{224,... | collective-permute-start | bytes 706568 | tf_op jit(solution)/shard_map/ppermute | solution.py:249
  25.9 0.0 collective-permute-done
  25.9 0.1 pad_maximum_fusion
  26.0 0.2 slice_subtract_fusion.1
  26.2 0.2 fusion.3
  26.4 0.2 slice_subtract_fusion.3
  26.6 9.6 %collective-permute-done.4 = f32[23,4,640]{2,1,0:T(4,128)S(1)} collective-permute-done((f32[23,4,640]{2,1,0:T(4,128)S(1)}, f32[23,4,640]{2,1,0:T(4,128)S(1)}, u32[]{:S(2)}, u32[]{:S(2)}) %collective-permute-start.4) | collective-permute-done | bytes 235552 | tf_op jit(solution)/shard_map/ppermute | solution.py:249
  36.2 0.0 copy-done
  36.2 0.3 fusion.13.refs_0_
  36.4 0.2 collective-permute-start.9
  36.6 1.5 %collective-permute-start.7 = (f32[23,4,640]{2,1,0:T(4,128)S(1)}, f32[23,4,640]{2,1,0:T(4,128)S(1)}, u32[]{:S(2)}, u32[]{:S(2)}) collective-permute-start(f32[23,4,640]{2,1,0:T(4,128)S(1)} %fusion.13.refs_0_), channel_id=1, source_target_pairs={{0,32},{32,0},{64,96},{96,64},{128,160},{160,128},{192,224},{224,1... | collective-permute-start | bytes 706568 | tf_op jit(solution)/shard_map/ppermute | solution.py:245
  38.1 2.5 %collective-permute-start.5 = (f32[23,4,640]{2,1,0:T(4,128)S(1)}, f32[23,4,640]{2,1,0:T(4,128)S(1)}, u32[]{:S(2)}, u32[]{:S(2)}) collective-permute-start(f32[23,4,640]{2,1,0:T(4,128)S(1)} %fusion.13.refs_0_), channel_id=1, source_target_pairs={{0,96},{32,64},{64,32},{96,0},{128,224},{160,192},{192,160},{224,1... | collective-permute-start | bytes 706568 | tf_op jit(solution)/shard_map/ppermute | solution.py:245
  40.6 6.1 %collective-permute-done.9.refs_0_ = f32[23,4,640]{2,1,0:T(4,128)S(1)} collective-permute-done((f32[23,4,640]{2,1,0:T(4,128)S(1)}, f32[23,4,640]{2,1,0:T(4,128)S(1)}, u32[]{:S(2)}, u32[]{:S(2)}) %collective-permute-start.9) | collective-permute-done | bytes 235552 | tf_op jit(solution)/shard_map/ppermute | solution.py:245
  46.7 1.6 %shard_map.62 = f32[23,4,640]{2,1,0:T(4,128)S(1)} custom-call(f32[23,4,640]{2,1,0:T(4,128)S(1)} %collective-permute-done.9.refs_0_, f32[23,16,640]{2,1,0:T(8,128)S(1)} %get-tuple-element.51.refs_1_, f32[23,16,640]{2,1,0:T(8,128)S(1)} %get-tuple-element.52.refs_2_, f32[23,16,640]{2,1,0:T(8,128)S(1)} %get-tuple-element.53.refs_3_), custom_call_target="tpu_custom_call" | custom-call | flops 9420800 | bytes 2826240 | tf_op jit(solution)/shard_map/pallas_call | solution.py:178
  48.3 0.2 collective-permute-start.10
  48.5 0.0 collective-permute-done.7.refs_0_
  48.5 1.6 %shard_map.60 = f32[23,4,640]{2,1,0:T(4,128)S(1)} custom-call(f32[23,4,640]{2,1,0:T(4,128)S(1)} %collective-permute-done.7.refs_0_, f32[23,16,640]{2,1,0:T(8,128)S(1)} %get-tuple-element.31.refs_4_.refs_1_, f32[23,16,640]{2,1,0:T(8,128)S(1)} %get-tuple-element.32.refs_5_.refs_2_, f32[23,16,640]{2,1,0:T(8,128)S(1)} %get-tuple-element.33.refs_6_.refs_3_), custom_call_target="tpu_custom_call" | custom-call | flops 9420800 | bytes 2826240 | tf_op jit(solution)/shard_map/pallas_call | solution.py:178
  50.1 2.0 %collective-permute-start.8 = (f32[23,4,640]{2,1,0:T(4,128)S(1)}, f32[23,4,640]{2,1,0:T(4,128)S(1)}, u32[]{:S(2)}, u32[]{:S(2)}) collective-permute-start(f32[23,4,640]{2,1,0:T(4,128)S(1)} %shard_map.60), channel_id=1, source_target_pairs={{0,32},{32,0},{64,96},{96,64},{128,160},{160,128},{192,224},{224,1... | collective-permute-start | bytes 706568 | tf_op jit(solution)/shard_map/ppermute | solution.py:245
  52.1 0.0 collective-permute-done.5.refs_0_
  52.1 1.6 %shard_map.61 = f32[23,4,640]{2,1,0:T(4,128)S(1)} custom-call(f32[23,4,640]{2,1,0:T(4,128)S(1)} %collective-permute-done.5.refs_0_, f32[23,16,640]{2,1,0:T(8,128)S(1)} %get-tuple-element.35.refs_4_.refs_1_, f32[23,16,640]{2,1,0:T(8,128)S(1)} %get-tuple-element.36.refs_5_.refs_2_, f32[23,16,640]{2,1,0:T(8,128)S(1)} %get-tuple-element.37.refs_6_.refs_3_), custom_call_target="tpu_custom_call" | custom-call | flops 9420800 | bytes 2826240 | tf_op jit(solution)/shard_map/pallas_call | solution.py:178
  53.6 1.5 %collective-permute-done.10 = f32[23,4,640]{2,1,0:T(4,128)S(1)} collective-permute-done((f32[23,4,640]{2,1,0:T(4,128)S(1)}, f32[23,4,640]{2,1,0:T(4,128)S(1)}, u32[]{:S(2)}, u32[]{:S(2)}) %collective-permute-start.10) | collective-permute-done | bytes 235552 | tf_op jit(solution)/shard_map/ppermute | solution.py:245
  55.2 0.1 add.82
  55.2 2.5 %collective-permute-start.11 = (f32[23,4,640]{2,1,0:T(4,128)S(1)}, f32[23,4,640]{2,1,0:T(4,128)S(1)}, u32[]{:S(2)}, u32[]{:S(2)}) collective-permute-start(f32[23,4,640]{2,1,0:T(4,128)S(1)} %add.82), channel_id=1, source_target_pairs={{0,96},{32,64},{64,32},{96,0},{128,224},{160,192},{192,160},{224,1... | collective-permute-start | bytes 706568 | tf_op jit(solution)/shard_map/ppermute | solution.py:245
  57.7 1.6 %shard_map.59 = f32[23,4,640]{2,1,0:T(4,128)S(1)} custom-call(f32[23,4,640]{2,1,0:T(4,128)S(1)} %fusion.13.refs_0_, f32[23,16,640]{2,1,0:T(8,128)S(1)} %get-tuple-element.42.refs_1_, f32[23,16,640]{2,1,0:T(8,128)S(1)} %get-tuple-element.43.refs_2_, f32[23,16,640]{2,1,0:T(8,128)S(1)} %get-tuple-element.44.refs_3_), custom_call_target="tpu_custom_call" | custom-call | flops 9420800 | bytes 2826240 | tf_op jit(solution)/shard_map/pallas_call | solution.py:178
  59.3 0.3 collective-permute-start.6
  59.6 0.0 collective-permute-done.8
  59.6 3.0 %collective-permute-done.11 = f32[23,4,640]{2,1,0:T(4,128)S(1)} collective-permute-done((f32[23,4,640]{2,1,0:T(4,128)S(1)}, f32[23,4,640]{2,1,0:T(4,128)S(1)}, u32[]{:S(2)}, u32[]{:S(2)}) %collective-permute-start.11) | collective-permute-done | bytes 235552 | tf_op jit(solution)/shard_map/ppermute | solution.py:245
  62.6 0.1 add_add_fusion
  62.7 5.0 %collective-permute-start.12 = (f32[23,4,640]{2,1,0:T(4,128)S(1)}, f32[23,4,640]{2,1,0:T(4,128)S(1)}, u32[]{:S(2)}, u32[]{:S(2)}) collective-permute-start(f32[23,4,640]{2,1,0:T(4,128)S(1)} %add_add_fusion), channel_id=1, source_target_pairs={{0,128},{32,160},{64,192},{96,224},{128,0},{160,32},{192,64},{224,... | collective-permute-start | bytes 706568 | tf_op jit(solution)/shard_map/ppermute | solution.py:249
  67.7 0.0 collective-permute-done.6
  67.8 0.1 pad_maximum_fusion.1
  67.8 0.2 slice_subtract_fusion
  68.0 0.2 fusion.1
  68.3 0.2 slice_subtract_fusion.2
  68.5 8.1 %collective-permute-done.12 = f32[23,4,640]{2,1,0:T(4,128)S(1)} collective-permute-done((f32[23,4,640]{2,1,0:T(4,128)S(1)}, f32[23,4,640]{2,1,0:T(4,128)S(1)}, u32[]{:S(2)}, u32[]{:S(2)}) %collective-permute-start.12) | collective-permute-done | bytes 235552 | tf_op jit(solution)/shard_map/ppermute | solution.py:249
  76.5 0.3 fusion.8.refs_0_
  76.8 0.1 collective-permute-start.15
  76.9 2.2 %collective-permute-start.14 = (f32[23,4,640]{2,1,0:T(4,128)S(1)}, f32[23,4,640]{2,1,0:T(4,128)S(1)}, u32[]{:S(2)}, u32[]{:S(2)}) collective-permute-start(f32[23,4,640]{2,1,0:T(4,128)S(1)} %fusion.8.refs_0_), channel_id=1, source_target_pairs={{0,64},{32,96},{64,0},{96,32},{128,192},{160,224},{192,128},{224,1... | collective-permute-start | bytes 706568 | tf_op jit(solution)/shard_map/ppermute | solution.py:245
  79.2 1.8 %collective-permute-start.13 = (f32[23,4,640]{2,1,0:T(4,128)S(1)}, f32[23,4,640]{2,1,0:T(4,128)S(1)}, u32[]{:S(2)}, u32[]{:S(2)}) collective-permute-start(f32[23,4,640]{2,1,0:T(4,128)S(1)} %fusion.8.refs_0_), channel_id=1, source_target_pairs={{0,32},{32,0},{64,96},{96,64},{128,160},{160,128},{192,224},{224,1... | collective-permute-start | bytes 706568 | tf_op jit(solution)/shard_map/ppermute | solution.py:245
  81.0 9.7 %collective-permute-done.15.refs_3_ = f32[23,4,640]{2,1,0:T(4,128)S(1)} collective-permute-done((f32[23,4,640]{2,1,0:T(4,128)S(1)}, f32[23,4,640]{2,1,0:T(4,128)S(1)}, u32[]{:S(2)}, u32[]{:S(2)}) %collective-permute-start.15) | collective-permute-done | bytes 235552 | tf_op jit(solution)/shard_map/ppermute | solution.py:245
  90.7 0.0 collective-permute-done.14.refs_2_
  90.7 0.6 collective-permute-done.13.refs_1_
  91.3 0.9 %join.1 = f32[90,4,640]{2,1,0:T(4,128)} custom-call(s32[1]{0:T(128)} %bitcast.at_y, f32[23,4,640]{2,1,0:T(4,128)S(1)} %fusion.8.refs_0_, f32[23,4,640]{2,1,0:T(4,128)S(1)} %collective-permute-done.13.refs_1_, f32[23,4,640]{2,1,0:T(4,128)S(1)} %collective-permute-done.14.refs_2_, f32[23,4,640]{2,1,0:T(4,128)S(1)} %collective-permute-done.15.refs_3_), custom_call_target="tpu_custom_call" | custom-call | tf_op jit(solution)/shard_map/join/pallas_call | solution.py:233
  (4 shorter events, 0.1 us)
Async XLA Ops:
  4.2 8.7 %collective-permute-start.2 = (f32[23,4,640]{2,1,0:T(4,128)S(1)}, f32[23,4,640]{2,1,0:T(4,128)S(1)}, u32[]{:S(2)}, u32[]{:S(2)}) collective-permute-start(f32[23,4,640]{2,1,0:T(4,128)S(1)} %get-tuple-element.47), channel_id=1, source_target_pairs={{0,32},{32,0},{64,96},{96,64},{128,160},{160,128},{192,224},{224,1... | collective-permute-start | bytes 706568 | tf_op jit(solution)/shard_map/ppermute | solution.py:245
  8.0 9.7 %collective-permute-start.1 = (f32[23,4,640]{2,1,0:T(4,128)S(1)}, f32[23,4,640]{2,1,0:T(4,128)S(1)}, u32[]{:S(2)}, u32[]{:S(2)}) collective-permute-start(f32[23,4,640]{2,1,0:T(4,128)S(1)} %get-tuple-element.45), channel_id=1, source_target_pairs={{0,32},{32,0},{64,96},{96,64},{128,160},{160,128},{192,224},{224,1... | collective-permute-start | bytes 706568 | tf_op jit(solution)/shard_map/ppermute | solution.py:245
  12.9 7.4 %collective-permute-start.3 = (f32[23,4,640]{2,1,0:T(4,128)S(1)}, f32[23,4,640]{2,1,0:T(4,128)S(1)}, u32[]{:S(2)}, u32[]{:S(2)}) collective-permute-start(f32[23,4,640]{2,1,0:T(4,128)S(1)} %add.74), channel_id=1, source_target_pairs={{0,96},{32,64},{64,32},{96,0},{128,224},{160,192},{192,160},{224,1... | collective-permute-start | bytes 706568 | tf_op jit(solution)/shard_map/ppermute | solution.py:245
  16.1 9.8 %collective-permute-start = (f32[2,4,640]{2,1,0:T(4,128)S(1)}, f32[2,4,640]{2,1,0:T(4,128)S(1)}, u32[]{:S(2)}, u32[]{:S(2)}) collective-permute-start(f32[2,4,640]{2,1,0:T(4,128)S(1)} %slice_select_fusion.3), channel_id=1, source_target_pairs={{0,1},{1,2},{2,3},{3,4},{4,5},{5,6},{6,7},{7,8},{8,9},{9,10},{10,1... | collective-permute-start | bytes 61448 | tf_op jit(solution)/shard_map/ppermute | solution.py:259
  16.1 20.1 %copy-start = (f32[4]{0:T(128)S(1)}, f32[4]{0:T(128)}, u32[]{:S(2)}) copy-start(f32[4]{0:T(128)} %constant.65) | copy-start | bytes 52
  20.4 15.8 %collective-permute-start.4 = (f32[23,4,640]{2,1,0:T(4,128)S(1)}, f32[23,4,640]{2,1,0:T(4,128)S(1)}, u32[]{:S(2)}, u32[]{:S(2)}) collective-permute-start(f32[23,4,640]{2,1,0:T(4,128)S(1)} %add_add_fusion.1), channel_id=1, source_target_pairs={{0,128},{32,160},{64,192},{96,224},{128,0},{160,32},{192,64},{224,... | collective-permute-start | bytes 706568 | tf_op jit(solution)/shard_map/ppermute | solution.py:249
  36.4 10.2 %collective-permute-start.9 = (f32[23,4,640]{2,1,0:T(4,128)S(1)}, f32[23,4,640]{2,1,0:T(4,128)S(1)}, u32[]{:S(2)}, u32[]{:S(2)}) collective-permute-start(f32[23,4,640]{2,1,0:T(4,128)S(1)} %fusion.13.refs_0_), channel_id=1, source_target_pairs={{0,64},{32,96},{64,0},{96,32},{128,192},{160,224},{192,128},{224,1... | collective-permute-start | bytes 706568 | tf_op jit(solution)/shard_map/ppermute | solution.py:245
  36.6 11.9 %collective-permute-start.7 = (f32[23,4,640]{2,1,0:T(4,128)S(1)}, f32[23,4,640]{2,1,0:T(4,128)S(1)}, u32[]{:S(2)}, u32[]{:S(2)}) collective-permute-start(f32[23,4,640]{2,1,0:T(4,128)S(1)} %fusion.13.refs_0_), channel_id=1, source_target_pairs={{0,32},{32,0},{64,96},{96,64},{128,160},{160,128},{192,224},{224,1... | collective-permute-start | bytes 706568 | tf_op jit(solution)/shard_map/ppermute | solution.py:245
  38.1 13.9 %collective-permute-start.5 = (f32[23,4,640]{2,1,0:T(4,128)S(1)}, f32[23,4,640]{2,1,0:T(4,128)S(1)}, u32[]{:S(2)}, u32[]{:S(2)}) collective-permute-start(f32[23,4,640]{2,1,0:T(4,128)S(1)} %fusion.13.refs_0_), channel_id=1, source_target_pairs={{0,96},{32,64},{64,32},{96,0},{128,224},{160,192},{192,160},{224,1... | collective-permute-start | bytes 706568 | tf_op jit(solution)/shard_map/ppermute | solution.py:245
  48.3 6.9 %collective-permute-start.10 = (f32[23,4,640]{2,1,0:T(4,128)S(1)}, f32[23,4,640]{2,1,0:T(4,128)S(1)}, u32[]{:S(2)}, u32[]{:S(2)}) collective-permute-start(f32[23,4,640]{2,1,0:T(4,128)S(1)} %shard_map.62), channel_id=1, source_target_pairs={{0,32},{32,0},{64,96},{96,64},{128,160},{160,128},{192,224},{224,1... | collective-permute-start | bytes 706568 | tf_op jit(solution)/shard_map/ppermute | solution.py:245
  50.1 9.5 %collective-permute-start.8 = (f32[23,4,640]{2,1,0:T(4,128)S(1)}, f32[23,4,640]{2,1,0:T(4,128)S(1)}, u32[]{:S(2)}, u32[]{:S(2)}) collective-permute-start(f32[23,4,640]{2,1,0:T(4,128)S(1)} %shard_map.60), channel_id=1, source_target_pairs={{0,32},{32,0},{64,96},{96,64},{128,160},{160,128},{192,224},{224,1... | collective-permute-start | bytes 706568 | tf_op jit(solution)/shard_map/ppermute | solution.py:245
  55.2 7.4 %collective-permute-start.11 = (f32[23,4,640]{2,1,0:T(4,128)S(1)}, f32[23,4,640]{2,1,0:T(4,128)S(1)}, u32[]{:S(2)}, u32[]{:S(2)}) collective-permute-start(f32[23,4,640]{2,1,0:T(4,128)S(1)} %add.82), channel_id=1, source_target_pairs={{0,96},{32,64},{64,32},{96,0},{128,224},{160,192},{192,160},{224,1... | collective-permute-start | bytes 706568 | tf_op jit(solution)/shard_map/ppermute | solution.py:245
  59.3 8.4 %collective-permute-start.6 = (f32[2,4,640]{2,1,0:T(4,128)S(1)}, f32[2,4,640]{2,1,0:T(4,128)S(1)}, u32[]{:S(2)}, u32[]{:S(2)}) collective-permute-start(f32[2,4,640]{2,1,0:T(4,128)S(1)} %slice_select_fusion.2), channel_id=1, source_target_pairs={{0,1},{1,2},{2,3},{3,4},{4,5},{5,6},{6,7},{7,8},{8,9},{9,10},{10,1... | collective-permute-start | bytes 61448 | tf_op jit(solution)/shard_map/ppermute | solution.py:259
  62.7 13.8 %collective-permute-start.12 = (f32[23,4,640]{2,1,0:T(4,128)S(1)}, f32[23,4,640]{2,1,0:T(4,128)S(1)}, u32[]{:S(2)}, u32[]{:S(2)}) collective-permute-start(f32[23,4,640]{2,1,0:T(4,128)S(1)} %add_add_fusion), channel_id=1, source_target_pairs={{0,128},{32,160},{64,192},{96,224},{128,0},{160,32},{192,64},{224,... | collective-permute-start | bytes 706568 | tf_op jit(solution)/shard_map/ppermute | solution.py:249
  76.8 13.9 %collective-permute-start.15 = (f32[23,4,640]{2,1,0:T(4,128)S(1)}, f32[23,4,640]{2,1,0:T(4,128)S(1)}, u32[]{:S(2)}, u32[]{:S(2)}) collective-permute-start(f32[23,4,640]{2,1,0:T(4,128)S(1)} %fusion.8.refs_0_), channel_id=1, source_target_pairs={{0,96},{32,64},{64,32},{96,0},{128,224},{160,192},{192,160},{224,1... | collective-permute-start | bytes 706568 | tf_op jit(solution)/shard_map/ppermute | solution.py:245
  76.9 13.8 %collective-permute-start.14 = (f32[23,4,640]{2,1,0:T(4,128)S(1)}, f32[23,4,640]{2,1,0:T(4,128)S(1)}, u32[]{:S(2)}, u32[]{:S(2)}) collective-permute-start(f32[23,4,640]{2,1,0:T(4,128)S(1)} %fusion.8.refs_0_), channel_id=1, source_target_pairs={{0,64},{32,96},{64,0},{96,32},{128,192},{160,224},{192,128},{224,1... | collective-permute-start | bytes 706568 | tf_op jit(solution)/shard_map/ppermute | solution.py:245
  79.2 12.2 %collective-permute-start.13 = (f32[23,4,640]{2,1,0:T(4,128)S(1)}, f32[23,4,640]{2,1,0:T(4,128)S(1)}, u32[]{:S(2)}, u32[]{:S(2)}) collective-permute-start(f32[23,4,640]{2,1,0:T(4,128)S(1)} %fusion.8.refs_0_), channel_id=1, source_target_pairs={{0,32},{32,0},{64,96},{96,64},{128,160},{160,128},{192,224},{224,1... | collective-permute-start | bytes 706568 | tf_op jit(solution)/shard_map/ppermute | solution.py:245

commit v4 on v3

--- a/solution.py
+++ b/solution.py
@@ -13,7 +13,7 @@
 SMOOTH = 0.03
 Y = 4
 ORDER = (2, 1, 3, 0)
-GROUP = 4
+GROUP = 8
 
 BEND = 0.33
 TAIL = (
@@ -221,7 +221,7 @@
 
 
 def later_steps(data, pieces):
-    for k in (0, 2, 1, 3):
+    for k in (0, 1, 3, 2):
         yield k, data[k], pieces[k], later_sums(data[k], pieces[k])
 
 
@@ -298,14 +298,15 @@
             made = first_sums(at_y, whole)
         sums, got = {}, {}
         for k, data[k], pieces[k], sums[k] in made:
-            if k == 2:
+            if k == 2 and step == 0:
                 relayed = swap_y(sums[2], 1)
-            elif k == 1:
-                got[1] = swap_y(sums[1], 1)
-            elif k == 3:
-                got[3] = swap_y(sums[3] + relayed, 3)
+            elif k:
+                out = sums[k] + relayed if k == 3 and step == 0 else sums[k]
+                got[k] = swap_y(out, k)
         edge = halo(flags, pieces[3])
         total = (sums[0] + got[1]) + got[3]
+        if step:
+            total = total + got[2]
         other = swap_z(total)
         edge = lax.optimization_barrier((edge, total))[0]
         base = smoothed(flags, pieces[0], pieces[1], pieces[3], edge, rows)

time: 93.8 us -> 92.3 us (0.984)
    ppermute x2, waiting for transfers between devices: 17.6 us -> 16.5 us  [swap_z(): lax.ppermute(block, 'tm', [(i, i ^ Y) for i in range(lax.axis_size('tm'))])]
where the time goes in v4:
time: 92.3 us; the launch traced here: 91.1 us
  waiting for transfers between devices  43.2 us (47%)
  starting transfers between devices  29 us (31%)
  Pallas kernels  16.5 us (18%)
  other arithmetic  2.18 us (2%)
    ppermute x12, waiting for transfers between devices, swap_y(): lax.ppermute(block, 'tm', [(i, i ^ k) for i in range(lax.axis_size('tm'))])  26.7 us
    ppermute x12, starting transfers between devices, swap_y(): lax.ppermute(block, 'tm', [(i, i ^ k) for i in range(lax.axis_size('tm'))])  18.2 us
    ppermute x2, waiting for transfers between devices, swap_z(): lax.ppermute(block, 'tm', [(i, i ^ Y) for i in range(lax.axis_size('tm'))])  16.5 us
    pallas_call x8, Pallas kernels, call(): pl.pallas_call(kernel, in_specs=in_specs, out_specs=[VMEM] * len(shapes),...  15.5 us
    ppermute x2, starting transfers between devices, swap_z(): lax.ppermute(block, 'tm', [(i, i ^ Y) for i in range(lax.axis_size('tm'))])  10.7 us
  transfers between devices with their start and end apart: 16, of which 9 were waited for; matrix products, arithmetic and copies ran while one was open for 2% of the time, Pallas kernels for 13%

profile of v4, /device:TPU:64, one launch (start us, length us, event | category | flops | bytes accessed | tf_op | source)
XLA Modules:
  0.0 91.1 jit_solution(7532930653861971342)
XLA Ops:
  0.0 4.1 %shard_map.55 = (f32[23,4,640]{2,1,0:T(4,128)S(1)}, f32[23,16,640]{2,1,0:T(8,128)S(1)}, f32[23,16,640]{2,1,0:T(8,128)S(1)}, f32[23,16,640]{2,1,0:T(8,128)S(1)}, ...) custom-call(s32[1]{0:T(128)} %bitcast.at_y, ...), custom_call_target="tpu_custom_call" | custom-call | flops 9420800 | bytes 2826240 | tf_op jit(solution)/shard_map/pallas_call | solution.py:178
  4.1 1.7 %collective-permute-start.2 = (f32[23,4,640]{2,1,0:T(4,128)S(1)}, f32[23,4,640]{2,1,0:T(4,128)S(1)}, u32[]{:S(2)}, u32[]{:S(2)}) collective-permute-start(f32[23,4,640]{2,1,0:T(4,128)S(1)} %get-tuple-element.47), channel_id=1, source_target_pairs={{0,32},{32,0},{64,96},{96,64},{128,160},{160,128},{192,224},{224,1... | collective-permute-start | bytes 706568 | tf_op jit(solution)/shard_map/ppermute | solution.py:245
  5.7 1.9 %shard_map.56 = (f32[23,4,640]{2,1,0:T(4,128)S(1)}, f32[23,16,640]{2,1,0:T(8,128)S(1)}, f32[23,16,640]{2,1,0:T(8,128)S(1)}, f32[23,16,640]{2,1,0:T(8,128)S(1)}, f32[23,4,640]{2,1,0:T(4,128)S(1)}) custom-call(s32[1]{0:T(128)} %bitcast.at_y, f32[90,16,640]{2,1,0:T(8,128)} %bitcast.7, f32[90,16,640]{2,1,0:T(8,128)} %bitcast.10, f32[90,16,640]{2,1,0:T(8,128)} %bitcast.13, ...), custom_call_target="tpu_custom_call" | custom-call | flops 9420800 | bytes 2826240 | tf_op jit(solution)/shard_map/pallas_call | solution.py:178
  7.6 0.5 collective-permute-start.1
  8.2 1.9 %shard_map.57 = (f32[23,4,640]{2,1,0:T(4,128)S(1)}, f32[23,16,640]{2,1,0:T(8,128)S(1)}, f32[23,16,640]{2,1,0:T(8,128)S(1)}, f32[23,16,640]{2,1,0:T(8,128)S(1)}, f32[23,4,640]{2,1,0:T(4,128)S(1)}) custom-call(s32[1]{0:T(128)} %bitcast.at_y, f32[90,16,640]{2,1,0:T(8,128)} %bitcast.8, f32[90,16,640]{2,1,0:T(8,128)} %bitcast.11, f32[90,16,640]{2,1,0:T(8,128)} %bitcast.14, ...), custom_call_target="tpu_custom_call" | custom-call | flops 9420800 | bytes 2826240 | tf_op jit(solution)/shard_map/pallas_call | solution.py:178
  10.1 2.7 %collective-permute-done.2 = f32[23,4,640]{2,1,0:T(4,128)S(1)} collective-permute-done((f32[23,4,640]{2,1,0:T(4,128)S(1)}, f32[23,4,640]{2,1,0:T(4,128)S(1)}, u32[]{:S(2)}, u32[]{:S(2)}) %collective-permute-start.2) | collective-permute-done | bytes 235552 | tf_op jit(solution)/shard_map/ppermute | solution.py:245
  12.8 0.1 add.74
  12.8 3.1 %collective-permute-start.3 = (f32[23,4,640]{2,1,0:T(4,128)S(1)}, f32[23,4,640]{2,1,0:T(4,128)S(1)}, u32[]{:S(2)}, u32[]{:S(2)}) collective-permute-start(f32[23,4,640]{2,1,0:T(4,128)S(1)} %add.74), channel_id=1, source_target_pairs={{0,96},{32,64},{64,32},{96,0},{128,224},{160,192},{192,160},{224,1... | collective-permute-start | bytes 706568 | tf_op jit(solution)/shard_map/ppermute | solution.py:245
  15.9 0.0 collective-permute-start
  15.9 0.0 copy-start
  16.0 1.5 %shard_map.58 = f32[23,4,640]{2,1,0:T(4,128)S(1)} custom-call(f32[23,4,640]{2,1,0:T(4,128)S(1)} %get-tuple-element.39.refs_0_, f32[23,16,640]{2,1,0:T(8,128)S(1)} %get-tuple-element.42.refs_1_, f32[23,16,640]{2,1,0:T(8,128)S(1)} %get-tuple-element.43.refs_2_, f32[23,16,640]{2,1,0:T(8,128)S(1)} %get-tuple-element.44.refs_3_), custom_call_target="tpu_custom_call" | custom-call | flops 9420800 | bytes 2826240 | tf_op jit(solution)/shard_map/pallas_call | solution.py:178
  17.5 0.0 collective-permute-done.1
  17.5 2.7 %collective-permute-done.3 = f32[23,4,640]{2,1,0:T(4,128)S(1)} collective-permute-done((f32[23,4,640]{2,1,0:T(4,128)S(1)}, f32[23,4,640]{2,1,0:T(4,128)S(1)}, u32[]{:S(2)}, u32[]{:S(2)}) %collective-permute-start.3) | collective-permute-done | bytes 235552 | tf_op jit(solution)/shard_map/ppermute | solution.py:245
  20.2 0.1 add_add_fusion.1
  20.3 5.5 %collective-permute-start.4 = (f32[23,4,640]{2,1,0:T(4,128)S(1)}, f32[23,4,640]{2,1,0:T(4,128)S(1)}, u32[]{:S(2)}, u32[]{:S(2)}) collective-permute-start(f32[23,4,640]{2,1,0:T(4,128)S(1)} %add_add_fusion.1), channel_id=1, source_target_pairs={{0,128},{32,160},{64,192},{96,224},{128,0},{160,32},{192,64},{224,... | collective-permute-start | bytes 706568 | tf_op jit(solution)/shard_map/ppermute | solution.py:249
  25.8 0.0 collective-permute-done
  25.8 0.1 pad_maximum_fusion
  25.9 0.2 slice_subtract_fusion.1
  26.1 0.2 fusion.3
  26.3 0.2 slice_subtract_fusion.3
  26.5 9.5 %collective-permute-done.4 = f32[23,4,640]{2,1,0:T(4,128)S(1)} collective-permute-done((f32[23,4,640]{2,1,0:T(4,128)S(1)}, f32[23,4,640]{2,1,0:T(4,128)S(1)}, u32[]{:S(2)}, u32[]{:S(2)}) %collective-permute-start.4) | collective-permute-done | bytes 235552 | tf_op jit(solution)/shard_map/ppermute | solution.py:249
  36.0 0.0 copy-done
  36.0 0.3 fusion.13.refs_0_
  36.3 0.2 collective-permute-start.10
  36.5 1.5 %collective-permute-start.7 = (f32[23,4,640]{2,1,0:T(4,128)S(1)}, f32[23,4,640]{2,1,0:T(4,128)S(1)}, u32[]{:S(2)}, u32[]{:S(2)}) collective-permute-start(f32[23,4,640]{2,1,0:T(4,128)S(1)} %fusion.13.refs_0_), channel_id=1, source_target_pairs={{0,32},{32,0},{64,96},{96,64},{128,160},{160,128},{192,224},{224,1... | collective-permute-start | bytes 706568 | tf_op jit(solution)/shard_map/ppermute | solution.py:245
  38.0 2.5 %collective-permute-start.5 = (f32[23,4,640]{2,1,0:T(4,128)S(1)}, f32[23,4,640]{2,1,0:T(4,128)S(1)}, u32[]{:S(2)}, u32[]{:S(2)}) collective-permute-start(f32[23,4,640]{2,1,0:T(4,128)S(1)} %fusion.13.refs_0_), channel_id=1, source_target_pairs={{0,96},{32,64},{64,32},{96,0},{128,224},{160,192},{192,160},{224,1... | collective-permute-start | bytes 706568 | tf_op jit(solution)/shard_map/ppermute | solution.py:245
  40.5 6.1 %collective-permute-done.10.refs_0_ = f32[23,4,640]{2,1,0:T(4,128)S(1)} collective-permute-done((f32[23,4,640]{2,1,0:T(4,128)S(1)}, f32[23,4,640]{2,1,0:T(4,128)S(1)}, u32[]{:S(2)}, u32[]{:S(2)}) %collective-permute-start.10) | collective-permute-done | bytes 235552 | tf_op jit(solution)/shard_map/ppermute | solution.py:245
  46.5 1.5 %shard_map.62 = f32[23,4,640]{2,1,0:T(4,128)S(1)} custom-call(f32[23,4,640]{2,1,0:T(4,128)S(1)} %collective-permute-done.10.refs_0_, f32[23,16,640]{2,1,0:T(8,128)S(1)} %get-tuple-element.51.refs_1_, f32[23,16,640]{2,1,0:T(8,128)S(1)} %get-tuple-element.52.refs_2_, f32[23,16,640]{2,1,0:T(8,128)S(1)} %get-tuple-element.53.refs_3_), custom_call_target="tpu_custom_call" | custom-call | flops 9420800 | bytes 2826240 | tf_op jit(solution)/shard_map/pallas_call | solution.py:178
  48.1 0.4 collective-permute-start.11
  48.5 0.0 collective-permute-done.7.refs_0_
  48.5 1.5 %shard_map.60 = f32[23,4,640]{2,1,0:T(4,128)S(1)} custom-call(f32[23,4,640]{2,1,0:T(4,128)S(1)} %collective-permute-done.7.refs_0_, f32[23,16,640]{2,1,0:T(8,128)S(1)} %get-tuple-element.31.refs_4_.refs_1_, f32[23,16,640]{2,1,0:T(8,128)S(1)} %get-tuple-element.32.refs_5_.refs_2_, f32[23,16,640]{2,1,0:T(8,128)S(1)} %get-tuple-element.33.refs_6_.refs_3_), custom_call_target="tpu_custom_call" | custom-call | flops 9420800 | bytes 2826240 | tf_op jit(solution)/shard_map/pallas_call | solution.py:178
  50.0 1.5 %collective-permute-start.8 = (f32[23,4,640]{2,1,0:T(4,128)S(1)}, f32[23,4,640]{2,1,0:T(4,128)S(1)}, u32[]{:S(2)}, u32[]{:S(2)}) collective-permute-start(f32[23,4,640]{2,1,0:T(4,128)S(1)} %shard_map.60), channel_id=1, source_target_pairs={{0,32},{32,0},{64,96},{96,64},{128,160},{160,128},{192,224},{224,1... | collective-permute-start | bytes 706568 | tf_op jit(solution)/shard_map/ppermute | solution.py:245
  51.5 0.0 collective-permute-done.5.refs_0_
  51.5 1.5 %shard_map.61 = f32[23,4,640]{2,1,0:T(4,128)S(1)} custom-call(f32[23,4,640]{2,1,0:T(4,128)S(1)} %collective-permute-done.5.refs_0_, f32[23,16,640]{2,1,0:T(8,128)S(1)} %get-tuple-element.35.refs_4_.refs_1_, f32[23,16,640]{2,1,0:T(8,128)S(1)} %get-tuple-element.36.refs_5_.refs_2_, f32[23,16,640]{2,1,0:T(8,128)S(1)} %get-tuple-element.37.refs_6_.refs_3_), custom_call_target="tpu_custom_call" | custom-call | flops 9420800 | bytes 2826240 | tf_op jit(solution)/shard_map/pallas_call | solution.py:178
  53.0 2.7 %collective-permute-start.9 = (f32[23,4,640]{2,1,0:T(4,128)S(1)}, f32[23,4,640]{2,1,0:T(4,128)S(1)}, u32[]{:S(2)}, u32[]{:S(2)}) collective-permute-start(f32[23,4,640]{2,1,0:T(4,128)S(1)} %shard_map.61), channel_id=1, source_target_pairs={{0,96},{32,64},{64,32},{96,0},{128,224},{160,192},{192,160},{224,1... | collective-permute-start | bytes 706568 | tf_op jit(solution)/shard_map/ppermute | solution.py:245
  55.7 1.5 %shard_map.59 = f32[23,4,640]{2,1,0:T(4,128)S(1)} custom-call(f32[23,4,640]{2,1,0:T(4,128)S(1)} %fusion.13.refs_0_, f32[23,16,640]{2,1,0:T(8,128)S(1)} %get-tuple-element.42.refs_1_, f32[23,16,640]{2,1,0:T(8,128)S(1)} %get-tuple-element.43.refs_2_, f32[23,16,640]{2,1,0:T(8,128)S(1)} %get-tuple-element.44.refs_3_), custom_call_target="tpu_custom_call" | custom-call | flops 9420800 | bytes 2826240 | tf_op jit(solution)/shard_map/pallas_call | solution.py:178
  57.2 0.1 collective-permute-start.6
  57.3 0.3 collective-permute-done.11
  57.6 0.0 collective-permute-done.8
  57.6 4.6 %collective-permute-done.9 = f32[23,4,640]{2,1,0:T(4,128)S(1)} collective-permute-done((f32[23,4,640]{2,1,0:T(4,128)S(1)}, f32[23,4,640]{2,1,0:T(4,128)S(1)}, u32[]{:S(2)}, u32[]{:S(2)}) %collective-permute-start.9) | collective-permute-done | bytes 235552 | tf_op jit(solution)/shard_map/ppermute | solution.py:245
  62.2 0.1 add_add_fusion
  62.3 5.2 %collective-permute-start.12 = (f32[23,4,640]{2,1,0:T(4,128)S(1)}, f32[23,4,640]{2,1,0:T(4,128)S(1)}, u32[]{:S(2)}, u32[]{:S(2)}) collective-permute-start(f32[23,4,640]{2,1,0:T(4,128)S(1)} %add_add_fusion), channel_id=1, source_target_pairs={{0,128},{32,160},{64,192},{96,224},{128,0},{160,32},{192,64},{224,... | collective-permute-start | bytes 706568 | tf_op jit(solution)/shard_map/ppermute | solution.py:249
  67.6 0.0 collective-permute-done.6
  67.6 0.1 pad_maximum_fusion.1
  67.7 0.2 slice_subtract_fusion
  67.9 0.2 fusion.1
  68.1 0.2 slice_subtract_fusion.2
  68.3 7.0 %collective-permute-done.12 = f32[23,4,640]{2,1,0:T(4,128)S(1)} collective-permute-done((f32[23,4,640]{2,1,0:T(4,128)S(1)}, f32[23,4,640]{2,1,0:T(4,128)S(1)}, u32[]{:S(2)}, u32[]{:S(2)}) %collective-permute-start.12) | collective-permute-done | bytes 235552 | tf_op jit(solution)/shard_map/ppermute | solution.py:249
  75.2 0.3 fusion.8.refs_0_
  75.5 0.4 collective-permute-start.15
  75.9 2.2 %collective-permute-start.14 = (f32[23,4,640]{2,1,0:T(4,128)S(1)}, f32[23,4,640]{2,1,0:T(4,128)S(1)}, u32[]{:S(2)}, u32[]{:S(2)}) collective-permute-start(f32[23,4,640]{2,1,0:T(4,128)S(1)} %fusion.8.refs_0_), channel_id=1, source_target_pairs={{0,64},{32,96},{64,0},{96,32},{128,192},{160,224},{192,128},{224,1... | collective-permute-start | bytes 706568 | tf_op jit(solution)/shard_map/ppermute | solution.py:245
  78.1 1.6 %collective-permute-start.13 = (f32[23,4,640]{2,1,0:T(4,128)S(1)}, f32[23,4,640]{2,1,0:T(4,128)S(1)}, u32[]{:S(2)}, u32[]{:S(2)}) collective-permute-start(f32[23,4,640]{2,1,0:T(4,128)S(1)} %fusion.8.refs_0_), channel_id=1, source_target_pairs={{0,32},{32,0},{64,96},{96,64},{128,160},{160,128},{192,224},{224,1... | collective-permute-start | bytes 706568 | tf_op jit(solution)/shard_map/ppermute | solution.py:245
  79.7 9.7 %collective-permute-done.15.refs_3_ = f32[23,4,640]{2,1,0:T(4,128)S(1)} collective-permute-done((f32[23,4,640]{2,1,0:T(4,128)S(1)}, f32[23,4,640]{2,1,0:T(4,128)S(1)}, u32[]{:S(2)}, u32[]{:S(2)}) %collective-permute-start.15) | collective-permute-done | bytes 235552 | tf_op jit(solution)/shard_map/ppermute | solution.py:245
  89.4 0.0 collective-permute-done.14.refs_2_
  89.4 0.6 collective-permute-done.13.refs_1_
  90.0 0.9 %join.1 = f32[90,4,640]{2,1,0:T(4,128)} custom-call(s32[1]{0:T(128)} %bitcast.at_y, f32[23,4,640]{2,1,0:T(4,128)S(1)} %fusion.8.refs_0_, f32[23,4,640]{2,1,0:T(4,128)S(1)} %collective-permute-done.13.refs_1_, f32[23,4,640]{2,1,0:T(4,128)S(1)} %collective-permute-done.14.refs_2_, f32[23,4,640]{2,1,0:T(4,128)S(1)} %collective-permute-done.15.refs_3_), custom_call_target="tpu_custom_call" | custom-call | tf_op jit(solution)/shard_map/join/pallas_call | solution.py:233
  (4 shorter events, 0.1 us)
Async XLA Ops:
  4.1 8.7 %collective-permute-start.2 = (f32[23,4,640]{2,1,0:T(4,128)S(1)}, f32[23,4,640]{2,1,0:T(4,128)S(1)}, u32[]{:S(2)}, u32[]{:S(2)}) collective-permute-start(f32[23,4,640]{2,1,0:T(4,128)S(1)} %get-tuple-element.47), channel_id=1, source_target_pairs={{0,32},{32,0},{64,96},{96,64},{128,160},{160,128},{192,224},{224,1... | collective-permute-start | bytes 706568 | tf_op jit(solution)/shard_map/ppermute | solution.py:245
  7.6 9.9 %collective-permute-start.1 = (f32[23,4,640]{2,1,0:T(4,128)S(1)}, f32[23,4,640]{2,1,0:T(4,128)S(1)}, u32[]{:S(2)}, u32[]{:S(2)}) collective-permute-start(f32[23,4,640]{2,1,0:T(4,128)S(1)} %get-tuple-element.45), channel_id=1, source_target_pairs={{0,32},{32,0},{64,96},{96,64},{128,160},{160,128},{192,224},{224,1... | collective-permute-start | bytes 706568 | tf_op jit(solution)/shard_map/ppermute | solution.py:245
  12.8 7.4 %collective-permute-start.3 = (f32[23,4,640]{2,1,0:T(4,128)S(1)}, f32[23,4,640]{2,1,0:T(4,128)S(1)}, u32[]{:S(2)}, u32[]{:S(2)}) collective-permute-start(f32[23,4,640]{2,1,0:T(4,128)S(1)} %add.74), channel_id=1, source_target_pairs={{0,96},{32,64},{64,32},{96,0},{128,224},{160,192},{192,160},{224,1... | collective-permute-start | bytes 706568 | tf_op jit(solution)/shard_map/ppermute | solution.py:245
  15.9 9.8 %collective-permute-start = (f32[2,4,640]{2,1,0:T(4,128)S(1)}, f32[2,4,640]{2,1,0:T(4,128)S(1)}, u32[]{:S(2)}, u32[]{:S(2)}) collective-permute-start(f32[2,4,640]{2,1,0:T(4,128)S(1)} %slice_select_fusion.3), channel_id=1, source_target_pairs={{0,1},{1,2},{2,3},{3,4},{4,5},{5,6},{6,7},{7,8},{8,9},{9,10},{10,1... | collective-permute-start | bytes 61448 | tf_op jit(solution)/shard_map/ppermute | solution.py:259
  15.9 20.1 %copy-start = (f32[4]{0:T(128)S(1)}, f32[4]{0:T(128)}, u32[]{:S(2)}) copy-start(f32[4]{0:T(128)} %constant.65) | copy-start | bytes 52
  20.3 15.7 %collective-permute-start.4 = (f32[23,4,640]{2,1,0:T(4,128)S(1)}, f32[23,4,640]{2,1,0:T(4,128)S(1)}, u32[]{:S(2)}, u32[]{:S(2)}) collective-permute-start(f32[23,4,640]{2,1,0:T(4,128)S(1)} %add_add_fusion.1), channel_id=1, source_target_pairs={{0,128},{32,160},{64,192},{96,224},{128,0},{160,32},{192,64},{224,... | collective-permute-start | bytes 706568 | tf_op jit(solution)/shard_map/ppermute | solution.py:249
  36.3 10.2 %collective-permute-start.10 = (f32[23,4,640]{2,1,0:T(4,128)S(1)}, f32[23,4,640]{2,1,0:T(4,128)S(1)}, u32[]{:S(2)}, u32[]{:S(2)}) collective-permute-start(f32[23,4,640]{2,1,0:T(4,128)S(1)} %fusion.13.refs_0_), channel_id=1, source_target_pairs={{0,64},{32,96},{64,0},{96,32},{128,192},{160,224},{192,128},{224,1... | collective-permute-start | bytes 706568 | tf_op jit(solution)/shard_map/ppermute | solution.py:245
  36.5 11.9 %collective-permute-start.7 = (f32[23,4,640]{2,1,0:T(4,128)S(1)}, f32[23,4,640]{2,1,0:T(4,128)S(1)}, u32[]{:S(2)}, u32[]{:S(2)}) collective-permute-start(f32[23,4,640]{2,1,0:T(4,128)S(1)} %fusion.13.refs_0_), channel_id=1, source_target_pairs={{0,32},{32,0},{64,96},{96,64},{128,160},{160,128},{192,224},{224,1... | collective-permute-start | bytes 706568 | tf_op jit(solution)/shard_map/ppermute | solution.py:245
  38.0 13.5 %collective-permute-start.5 = (f32[23,4,640]{2,1,0:T(4,128)S(1)}, f32[23,4,640]{2,1,0:T(4,128)S(1)}, u32[]{:S(2)}, u32[]{:S(2)}) collective-permute-start(f32[23,4,640]{2,1,0:T(4,128)S(1)} %fusion.13.refs_0_), channel_id=1, source_target_pairs={{0,96},{32,64},{64,32},{96,0},{128,224},{160,192},{192,160},{224,1... | collective-permute-start | bytes 706568 | tf_op jit(solution)/shard_map/ppermute | solution.py:245
  48.1 9.5 %collective-permute-start.11 = (f32[23,4,640]{2,1,0:T(4,128)S(1)}, f32[23,4,640]{2,1,0:T(4,128)S(1)}, u32[]{:S(2)}, u32[]{:S(2)}) collective-permute-start(f32[23,4,640]{2,1,0:T(4,128)S(1)} %shard_map.62), channel_id=1, source_target_pairs={{0,64},{32,96},{64,0},{96,32},{128,192},{160,224},{192,128},{224,1... | collective-permute-start | bytes 706568 | tf_op jit(solution)/shard_map/ppermute | solution.py:245
  50.0 7.6 %collective-permute-start.8 = (f32[23,4,640]{2,1,0:T(4,128)S(1)}, f32[23,4,640]{2,1,0:T(4,128)S(1)}, u32[]{:S(2)}, u32[]{:S(2)}) collective-permute-start(f32[23,4,640]{2,1,0:T(4,128)S(1)} %shard_map.60), channel_id=1, source_target_pairs={{0,32},{32,0},{64,96},{96,64},{128,160},{160,128},{192,224},{224,1... | collective-permute-start | bytes 706568 | tf_op jit(solution)/shard_map/ppermute | solution.py:245
  53.0 9.2 %collective-permute-start.9 = (f32[23,4,640]{2,1,0:T(4,128)S(1)}, f32[23,4,640]{2,1,0:T(4,128)S(1)}, u32[]{:S(2)}, u32[]{:S(2)}) collective-permute-start(f32[23,4,640]{2,1,0:T(4,128)S(1)} %shard_map.61), channel_id=1, source_target_pairs={{0,96},{32,64},{64,32},{96,0},{128,224},{160,192},{192,160},{224,1... | collective-permute-start | bytes 706568 | tf_op jit(solution)/shard_map/ppermute | solution.py:245
  57.2 10.3 %collective-permute-start.6 = (f32[2,4,640]{2,1,0:T(4,128)S(1)}, f32[2,4,640]{2,1,0:T(4,128)S(1)}, u32[]{:S(2)}, u32[]{:S(2)}) collective-permute-start(f32[2,4,640]{2,1,0:T(4,128)S(1)} %slice_select_fusion.2), channel_id=1, source_target_pairs={{0,1},{1,2},{2,3},{3,4},{4,5},{5,6},{6,7},{7,8},{8,9},{9,10},{10,1... | collective-permute-start | bytes 61448 | tf_op jit(solution)/shard_map/ppermute | solution.py:259
  62.3 12.9 %collective-permute-start.12 = (f32[23,4,640]{2,1,0:T(4,128)S(1)}, f32[23,4,640]{2,1,0:T(4,128)S(1)}, u32[]{:S(2)}, u32[]{:S(2)}) collective-permute-start(f32[23,4,640]{2,1,0:T(4,128)S(1)} %add_add_fusion), channel_id=1, source_target_pairs={{0,128},{32,160},{64,192},{96,224},{128,0},{160,32},{192,64},{224,... | collective-permute-start | bytes 706568 | tf_op jit(solution)/shard_map/ppermute | solution.py:249
  75.5 13.9 %collective-permute-start.15 = (f32[23,4,640]{2,1,0:T(4,128)S(1)}, f32[23,4,640]{2,1,0:T(4,128)S(1)}, u32[]{:S(2)}, u32[]{:S(2)}) collective-permute-start(f32[23,4,640]{2,1,0:T(4,128)S(1)} %fusion.8.refs_0_), channel_id=1, source_target_pairs={{0,96},{32,64},{64,32},{96,0},{128,224},{160,192},{192,160},{224,1... | collective-permute-start | bytes 706568 | tf_op jit(solution)/shard_map/ppermute | solution.py:245
  75.9 13.5 %collective-permute-start.14 = (f32[23,4,640]{2,1,0:T(4,128)S(1)}, f32[23,4,640]{2,1,0:T(4,128)S(1)}, u32[]{:S(2)}, u32[]{:S(2)}) collective-permute-start(f32[23,4,640]{2,1,0:T(4,128)S(1)} %fusion.8.refs_0_), channel_id=1, source_target_pairs={{0,64},{32,96},{64,0},{96,32},{128,192},{160,224},{192,128},{224,1... | collective-permute-start | bytes 706568 | tf_op jit(solution)/shard_map/ppermute | solution.py:245
  78.1 11.9 %collective-permute-start.13 = (f32[23,4,640]{2,1,0:T(4,128)S(1)}, f32[23,4,640]{2,1,0:T(4,128)S(1)}, u32[]{:S(2)}, u32[]{:S(2)}) collective-permute-start(f32[23,4,640]{2,1,0:T(4,128)S(1)} %fusion.8.refs_0_), channel_id=1, source_target_pairs={{0,32},{32,0},{64,96},{96,64},{128,160},{160,128},{192,224},{224,1... | collective-permute-start | bytes 706568 | tf_op jit(solution)/shard_map/ppermute | solution.py:245

commit v5 on v4

--- a/solution.py
+++ b/solution.py
@@ -14,6 +14,7 @@
 Y = 4
 ORDER = (2, 1, 3, 0)
 GROUP = 8
+LOOP = 12
 
 BEND = 0.33
 TAIL = (
@@ -72,20 +73,21 @@
 
 def sum_rows(refs, ready=None):
     tall = refs[-1].shape[0]
-    turns = tall // GROUP
+    size = LOOP if ready is None else GROUP
+    turns = tall // size
 
     def turn(i, carry):
         if ready is not None:
-            ready(i * GROUP, GROUP, i)
-        for n in range(GROUP):
-            sum_row(*refs, i * GROUP + n)
+            ready(i * size, size, i)
+        for n in range(size):
+            sum_row(*refs, i * size + n)
         return carry
 
     lax.fori_loop(0, turns, turn, 0)
-    if tall % GROUP:
+    if tall % size:
         if ready is not None:
-            ready(turns * GROUP, tall % GROUP, turns)
-        for n in range(turns * GROUP, tall):
+            ready(turns * size, tall % size, turns)
+        for n in range(turns * size, tall):
             sum_row(*refs, n)
 
 

time: 92.3 us -> 92 us (level)
  transfers between devices with their start and end apart: 16 -> 16, of which waited for: 9 -> 9; matrix products, arithmetic and copies ran while one was open for 2% -> 2% of each run, Pallas kernels for 13% -> 12%
where the time goes in v5:
time: 92 us; the launch traced here: 91.3 us
  waiting for transfers between devices  43.6 us (47%)
  starting transfers between devices  28.8 us (31%)
  Pallas kernels  16.3 us (18%)
  other arithmetic  2.18 us (2%)
    ppermute x12, waiting for transfers between devices, swap_y(): lax.ppermute(block, 'tm', [(i, i ^ k) for i in range(lax.axis_size('tm'))])  27 us
    ppermute x12, starting transfers between devices, swap_y(): lax.ppermute(block, 'tm', [(i, i ^ k) for i in range(lax.axis_size('tm'))])  18 us
    ppermute x2, waiting for transfers between devices, swap_z(): lax.ppermute(block, 'tm', [(i, i ^ Y) for i in range(lax.axis_size('tm'))])  16.6 us
    pallas_call x8, Pallas kernels, call(): pl.pallas_call(kernel, in_specs=in_specs, out_specs=[VMEM] * len(shapes),...  15.4 us
    ppermute x2, starting transfers between devices, swap_z(): lax.ppermute(block, 'tm', [(i, i ^ Y) for i in range(lax.axis_size('tm'))])  10.7 us
  transfers between devices with their start and end apart: 16, of which 9 were waited for; matrix products, arithmetic and copies ran while one was open for 2% of the time, Pallas kernels for 12%

profile of v5, /device:TPU:64, one launch (start us, length us, event | category | flops | bytes accessed | tf_op | source)
XLA Modules:
  0.0 91.3 jit_solution(17180054667136151848)
XLA Ops:
  0.0 4.1 %shard_map.55 = (f32[23,4,640]{2,1,0:T(4,128)S(1)}, f32[23,16,640]{2,1,0:T(8,128)S(1)}, f32[23,16,640]{2,1,0:T(8,128)S(1)}, f32[23,16,640]{2,1,0:T(8,128)S(1)}, ...) custom-call(s32[1]{0:T(128)} %bitcast.at_y, ...), custom_call_target="tpu_custom_call" | custom-call | flops 9420800 | bytes 2826240 | tf_op jit(solution)/shard_map/pallas_call | solution.py:180
  4.1 1.7 %collective-permute-start.2 = (f32[23,4,640]{2,1,0:T(4,128)S(1)}, f32[23,4,640]{2,1,0:T(4,128)S(1)}, u32[]{:S(2)}, u32[]{:S(2)}) collective-permute-start(f32[23,4,640]{2,1,0:T(4,128)S(1)} %get-tuple-element.47), channel_id=1, source_target_pairs={{0,32},{32,0},{64,96},{96,64},{128,160},{160,128},{192,224},{224,1... | collective-permute-start | bytes 706568 | tf_op jit(solution)/shard_map/ppermute | solution.py:247
  5.7 1.9 %shard_map.56 = (f32[23,4,640]{2,1,0:T(4,128)S(1)}, f32[23,16,640]{2,1,0:T(8,128)S(1)}, f32[23,16,640]{2,1,0:T(8,128)S(1)}, f32[23,16,640]{2,1,0:T(8,128)S(1)}, f32[23,4,640]{2,1,0:T(4,128)S(1)}) custom-call(s32[1]{0:T(128)} %bitcast.at_y, f32[90,16,640]{2,1,0:T(8,128)} %bitcast.7, f32[90,16,640]{2,1,0:T(8,128)} %bitcast.10, f32[90,16,640]{2,1,0:T(8,128)} %bitcast.13, ...), custom_call_target="tpu_custom_call" | custom-call | flops 9420800 | bytes 2826240 | tf_op jit(solution)/shard_map/pallas_call | solution.py:180
  7.6 0.5 collective-permute-start.1
  8.2 1.9 %shard_map.57 = (f32[23,4,640]{2,1,0:T(4,128)S(1)}, f32[23,16,640]{2,1,0:T(8,128)S(1)}, f32[23,16,640]{2,1,0:T(8,128)S(1)}, f32[23,16,640]{2,1,0:T(8,128)S(1)}, f32[23,4,640]{2,1,0:T(4,128)S(1)}) custom-call(s32[1]{0:T(128)} %bitcast.at_y, f32[90,16,640]{2,1,0:T(8,128)} %bitcast.8, f32[90,16,640]{2,1,0:T(8,128)} %bitcast.11, f32[90,16,640]{2,1,0:T(8,128)} %bitcast.14, ...), custom_call_target="tpu_custom_call" | custom-call | flops 9420800 | bytes 2826240 | tf_op jit(solution)/shard_map/pallas_call | solution.py:180
  10.1 2.7 %collective-permute-done.2 = f32[23,4,640]{2,1,0:T(4,128)S(1)} collective-permute-done((f32[23,4,640]{2,1,0:T(4,128)S(1)}, f32[23,4,640]{2,1,0:T(4,128)S(1)}, u32[]{:S(2)}, u32[]{:S(2)}) %collective-permute-start.2) | collective-permute-done | bytes 235552 | tf_op jit(solution)/shard_map/ppermute | solution.py:247
  12.8 0.1 add.74
  12.8 3.1 %collective-permute-start.3 = (f32[23,4,640]{2,1,0:T(4,128)S(1)}, f32[23,4,640]{2,1,0:T(4,128)S(1)}, u32[]{:S(2)}, u32[]{:S(2)}) collective-permute-start(f32[23,4,640]{2,1,0:T(4,128)S(1)} %add.74), channel_id=1, source_target_pairs={{0,96},{32,64},{64,32},{96,0},{128,224},{160,192},{192,160},{224,1... | collective-permute-start | bytes 706568 | tf_op jit(solution)/shard_map/ppermute | solution.py:247
  15.9 0.0 collective-permute-start
  15.9 0.0 copy-start
  16.0 1.5 %shard_map.58 = f32[23,4,640]{2,1,0:T(4,128)S(1)} custom-call(f32[23,4,640]{2,1,0:T(4,128)S(1)} %get-tuple-element.39.refs_0_, f32[23,16,640]{2,1,0:T(8,128)S(1)} %get-tuple-element.42.refs_1_, f32[23,16,640]{2,1,0:T(8,128)S(1)} %get-tuple-element.43.refs_2_, f32[23,16,640]{2,1,0:T(8,128)S(1)} %get-tuple-element.44.refs_3_), custom_call_target="tpu_custom_call" | custom-call | flops 9420800 | bytes 2826240 | tf_op jit(solution)/shard_map/pallas_call | solution.py:180
  17.5 0.0 collective-permute-done.1
  17.5 2.7 %collective-permute-done.3 = f32[23,4,640]{2,1,0:T(4,128)S(1)} collective-permute-done((f32[23,4,640]{2,1,0:T(4,128)S(1)}, f32[23,4,640]{2,1,0:T(4,128)S(1)}, u32[]{:S(2)}, u32[]{:S(2)}) %collective-permute-start.3) | collective-permute-done | bytes 235552 | tf_op jit(solution)/shard_map/ppermute | solution.py:247
  20.2 0.1 add_add_fusion.1
  20.3 5.5 %collective-permute-start.4 = (f32[23,4,640]{2,1,0:T(4,128)S(1)}, f32[23,4,640]{2,1,0:T(4,128)S(1)}, u32[]{:S(2)}, u32[]{:S(2)}) collective-permute-start(f32[23,4,640]{2,1,0:T(4,128)S(1)} %add_add_fusion.1), channel_id=1, source_target_pairs={{0,128},{32,160},{64,192},{96,224},{128,0},{160,32},{192,64},{224,... | collective-permute-start | bytes 706568 | tf_op jit(solution)/shard_map/ppermute | solution.py:251
  25.8 0.0 collective-permute-done
  25.8 0.1 pad_maximum_fusion
  25.9 0.2 slice_subtract_fusion.1
  26.1 0.2 fusion.3
  26.3 0.2 slice_subtract_fusion.3
  26.5 9.5 %collective-permute-done.4 = f32[23,4,640]{2,1,0:T(4,128)S(1)} collective-permute-done((f32[23,4,640]{2,1,0:T(4,128)S(1)}, f32[23,4,640]{2,1,0:T(4,128)S(1)}, u32[]{:S(2)}, u32[]{:S(2)}) %collective-permute-start.4) | collective-permute-done | bytes 235552 | tf_op jit(solution)/shard_map/ppermute | solution.py:251
  36.0 0.0 copy-done
  36.0 0.3 fusion.13.refs_0_
  36.3 0.3 collective-permute-start.10
  36.5 1.5 %collective-permute-start.7 = (f32[23,4,640]{2,1,0:T(4,128)S(1)}, f32[23,4,640]{2,1,0:T(4,128)S(1)}, u32[]{:S(2)}, u32[]{:S(2)}) collective-permute-start(f32[23,4,640]{2,1,0:T(4,128)S(1)} %fusion.13.refs_0_), channel_id=1, source_target_pairs={{0,32},{32,0},{64,96},{96,64},{128,160},{160,128},{192,224},{224,1... | collective-permute-start | bytes 706568 | tf_op jit(solution)/shard_map/ppermute | solution.py:247
  38.0 2.4 %collective-permute-start.5 = (f32[23,4,640]{2,1,0:T(4,128)S(1)}, f32[23,4,640]{2,1,0:T(4,128)S(1)}, u32[]{:S(2)}, u32[]{:S(2)}) collective-permute-start(f32[23,4,640]{2,1,0:T(4,128)S(1)} %fusion.13.refs_0_), channel_id=1, source_target_pairs={{0,96},{32,64},{64,32},{96,0},{128,224},{160,192},{192,160},{224,1... | collective-permute-start | bytes 706568 | tf_op jit(solution)/shard_map/ppermute | solution.py:247
  40.4 6.1 %collective-permute-done.10.refs_0_ = f32[23,4,640]{2,1,0:T(4,128)S(1)} collective-permute-done((f32[23,4,640]{2,1,0:T(4,128)S(1)}, f32[23,4,640]{2,1,0:T(4,128)S(1)}, u32[]{:S(2)}, u32[]{:S(2)}) %collective-permute-start.10) | collective-permute-done | bytes 235552 | tf_op jit(solution)/shard_map/ppermute | solution.py:247
  46.5 1.5 %shard_map.62 = f32[23,4,640]{2,1,0:T(4,128)S(1)} custom-call(f32[23,4,640]{2,1,0:T(4,128)S(1)} %collective-permute-done.10.refs_0_, f32[23,16,640]{2,1,0:T(8,128)S(1)} %get-tuple-element.51.refs_1_, f32[23,16,640]{2,1,0:T(8,128)S(1)} %get-tuple-element.52.refs_2_, f32[23,16,640]{2,1,0:T(8,128)S(1)} %get-tuple-element.53.refs_3_), custom_call_target="tpu_custom_call" | custom-call | flops 9420800 | bytes 2826240 | tf_op jit(solution)/shard_map/pallas_call | solution.py:180
  48.0 0.2 collective-permute-start.11
  48.2 0.0 collective-permute-done.7.refs_0_
  48.2 1.5 %shard_map.60 = f32[23,4,640]{2,1,0:T(4,128)S(1)} custom-call(f32[23,4,640]{2,1,0:T(4,128)S(1)} %collective-permute-done.7.refs_0_, f32[23,16,640]{2,1,0:T(8,128)S(1)} %get-tuple-element.31.refs_4_.refs_1_, f32[23,16,640]{2,1,0:T(8,128)S(1)} %get-tuple-element.32.refs_5_.refs_2_, f32[23,16,640]{2,1,0:T(8,128)S(1)} %get-tuple-element.33.refs_6_.refs_3_), custom_call_target="tpu_custom_call" | custom-call | flops 9420800 | bytes 2826240 | tf_op jit(solution)/shard_map/pallas_call | solution.py:180
  49.7 1.5 %collective-permute-start.8 = (f32[23,4,640]{2,1,0:T(4,128)S(1)}, f32[23,4,640]{2,1,0:T(4,128)S(1)}, u32[]{:S(2)}, u32[]{:S(2)}) collective-permute-start(f32[23,4,640]{2,1,0:T(4,128)S(1)} %shard_map.60), channel_id=1, source_target_pairs={{0,32},{32,0},{64,96},{96,64},{128,160},{160,128},{192,224},{224,1... | collective-permute-start | bytes 706568 | tf_op jit(solution)/shard_map/ppermute | solution.py:247
  51.2 0.0 collective-permute-done.5.refs_0_
  51.2 1.5 %shard_map.61 = f32[23,4,640]{2,1,0:T(4,128)S(1)} custom-call(f32[23,4,640]{2,1,0:T(4,128)S(1)} %collective-permute-done.5.refs_0_, f32[23,16,640]{2,1,0:T(8,128)S(1)} %get-tuple-element.35.refs_4_.refs_1_, f32[23,16,640]{2,1,0:T(8,128)S(1)} %get-tuple-element.36.refs_5_.refs_2_, f32[23,16,640]{2,1,0:T(8,128)S(1)} %get-tuple-element.37.refs_6_.refs_3_), custom_call_target="tpu_custom_call" | custom-call | flops 9420800 | bytes 2826240 | tf_op jit(solution)/shard_map/pallas_call | solution.py:180
  52.7 2.6 %collective-permute-start.9 = (f32[23,4,640]{2,1,0:T(4,128)S(1)}, f32[23,4,640]{2,1,0:T(4,128)S(1)}, u32[]{:S(2)}, u32[]{:S(2)}) collective-permute-start(f32[23,4,640]{2,1,0:T(4,128)S(1)} %shard_map.61), channel_id=1, source_target_pairs={{0,96},{32,64},{64,32},{96,0},{128,224},{160,192},{192,160},{224,1... | collective-permute-start | bytes 706568 | tf_op jit(solution)/shard_map/ppermute | solution.py:247
  55.4 1.5 %shard_map.59 = f32[23,4,640]{2,1,0:T(4,128)S(1)} custom-call(f32[23,4,640]{2,1,0:T(4,128)S(1)} %fusion.13.refs_0_, f32[23,16,640]{2,1,0:T(8,128)S(1)} %get-tuple-element.42.refs_1_, f32[23,16,640]{2,1,0:T(8,128)S(1)} %get-tuple-element.43.refs_2_, f32[23,16,640]{2,1,0:T(8,128)S(1)} %get-tuple-element.44.refs_3_), custom_call_target="tpu_custom_call" | custom-call | flops 9420800 | bytes 2826240 | tf_op jit(solution)/shard_map/pallas_call | solution.py:180
  56.9 0.1 collective-permute-start.6
  57.0 0.5 collective-permute-done.11
  57.5 0.0 collective-permute-done.8
  57.5 4.6 %collective-permute-done.9 = f32[23,4,640]{2,1,0:T(4,128)S(1)} collective-permute-done((f32[23,4,640]{2,1,0:T(4,128)S(1)}, f32[23,4,640]{2,1,0:T(4,128)S(1)}, u32[]{:S(2)}, u32[]{:S(2)}) %collective-permute-start.9) | collective-permute-done | bytes 235552 | tf_op jit(solution)/shard_map/ppermute | solution.py:247
  62.2 0.1 add_add_fusion
  62.3 5.2 %collective-permute-start.12 = (f32[23,4,640]{2,1,0:T(4,128)S(1)}, f32[23,4,640]{2,1,0:T(4,128)S(1)}, u32[]{:S(2)}, u32[]{:S(2)}) collective-permute-start(f32[23,4,640]{2,1,0:T(4,128)S(1)} %add_add_fusion), channel_id=1, source_target_pairs={{0,128},{32,160},{64,192},{96,224},{128,0},{160,32},{192,64},{224,... | collective-permute-start | bytes 706568 | tf_op jit(solution)/shard_map/ppermute | solution.py:251
  67.5 0.0 collective-permute-done.6
  67.5 0.1 pad_maximum_fusion.1
  67.6 0.2 slice_subtract_fusion
  67.8 0.2 fusion.1
  68.0 0.2 slice_subtract_fusion.2
  68.2 7.1 %collective-permute-done.12 = f32[23,4,640]{2,1,0:T(4,128)S(1)} collective-permute-done((f32[23,4,640]{2,1,0:T(4,128)S(1)}, f32[23,4,640]{2,1,0:T(4,128)S(1)}, u32[]{:S(2)}, u32[]{:S(2)}) %collective-permute-start.12) | collective-permute-done | bytes 235552 | tf_op jit(solution)/shard_map/ppermute | solution.py:251
  75.4 0.3 fusion.8.refs_0_
  75.6 0.5 collective-permute-start.15
  76.1 2.2 %collective-permute-start.14 = (f32[23,4,640]{2,1,0:T(4,128)S(1)}, f32[23,4,640]{2,1,0:T(4,128)S(1)}, u32[]{:S(2)}, u32[]{:S(2)}) collective-permute-start(f32[23,4,640]{2,1,0:T(4,128)S(1)} %fusion.8.refs_0_), channel_id=1, source_target_pairs={{0,64},{32,96},{64,0},{96,32},{128,192},{160,224},{192,128},{224,1... | collective-permute-start | bytes 706568 | tf_op jit(solution)/shard_map/ppermute | solution.py:247
  78.2 1.6 %collective-permute-start.13 = (f32[23,4,640]{2,1,0:T(4,128)S(1)}, f32[23,4,640]{2,1,0:T(4,128)S(1)}, u32[]{:S(2)}, u32[]{:S(2)}) collective-permute-start(f32[23,4,640]{2,1,0:T(4,128)S(1)} %fusion.8.refs_0_), channel_id=1, source_target_pairs={{0,32},{32,0},{64,96},{96,64},{128,160},{160,128},{192,224},{224,1... | collective-permute-start | bytes 706568 | tf_op jit(solution)/shard_map/ppermute | solution.py:247
  79.8 9.7 %collective-permute-done.15.refs_3_ = f32[23,4,640]{2,1,0:T(4,128)S(1)} collective-permute-done((f32[23,4,640]{2,1,0:T(4,128)S(1)}, f32[23,4,640]{2,1,0:T(4,128)S(1)}, u32[]{:S(2)}, u32[]{:S(2)}) %collective-permute-start.15) | collective-permute-done | bytes 235552 | tf_op jit(solution)/shard_map/ppermute | solution.py:247
  89.5 0.0 collective-permute-done.14.refs_2_
  89.5 0.6 collective-permute-done.13.refs_1_
  90.1 0.9 %join.1 = f32[90,4,640]{2,1,0:T(4,128)} custom-call(s32[1]{0:T(128)} %bitcast.at_y, f32[23,4,640]{2,1,0:T(4,128)S(1)} %fusion.8.refs_0_, f32[23,4,640]{2,1,0:T(4,128)S(1)} %collective-permute-done.13.refs_1_, f32[23,4,640]{2,1,0:T(4,128)S(1)} %collective-permute-done.14.refs_2_, f32[23,4,640]{2,1,0:T(4,128)S(1)} %collective-permute-done.15.refs_3_), custom_call_target="tpu_custom_call" | custom-call | tf_op jit(solution)/shard_map/join/pallas_call | solution.py:235
  (4 shorter events, 0.1 us)
Async XLA Ops:
  4.1 8.7 %collective-permute-start.2 = (f32[23,4,640]{2,1,0:T(4,128)S(1)}, f32[23,4,640]{2,1,0:T(4,128)S(1)}, u32[]{:S(2)}, u32[]{:S(2)}) collective-permute-start(f32[23,4,640]{2,1,0:T(4,128)S(1)} %get-tuple-element.47), channel_id=1, source_target_pairs={{0,32},{32,0},{64,96},{96,64},{128,160},{160,128},{192,224},{224,1... | collective-permute-start | bytes 706568 | tf_op jit(solution)/shard_map/ppermute | solution.py:247
  7.6 9.8 %collective-permute-start.1 = (f32[23,4,640]{2,1,0:T(4,128)S(1)}, f32[23,4,640]{2,1,0:T(4,128)S(1)}, u32[]{:S(2)}, u32[]{:S(2)}) collective-permute-start(f32[23,4,640]{2,1,0:T(4,128)S(1)} %get-tuple-element.45), channel_id=1, source_target_pairs={{0,32},{32,0},{64,96},{96,64},{128,160},{160,128},{192,224},{224,1... | collective-permute-start | bytes 706568 | tf_op jit(solution)/shard_map/ppermute | solution.py:247
  12.8 7.4 %collective-permute-start.3 = (f32[23,4,640]{2,1,0:T(4,128)S(1)}, f32[23,4,640]{2,1,0:T(4,128)S(1)}, u32[]{:S(2)}, u32[]{:S(2)}) collective-permute-start(f32[23,4,640]{2,1,0:T(4,128)S(1)} %add.74), channel_id=1, source_target_pairs={{0,96},{32,64},{64,32},{96,0},{128,224},{160,192},{192,160},{224,1... | collective-permute-start | bytes 706568 | tf_op jit(solution)/shard_map/ppermute | solution.py:247
  15.9 9.8 %collective-permute-start = (f32[2,4,640]{2,1,0:T(4,128)S(1)}, f32[2,4,640]{2,1,0:T(4,128)S(1)}, u32[]{:S(2)}, u32[]{:S(2)}) collective-permute-start(f32[2,4,640]{2,1,0:T(4,128)S(1)} %slice_select_fusion.3), channel_id=1, source_target_pairs={{0,1},{1,2},{2,3},{3,4},{4,5},{5,6},{6,7},{7,8},{8,9},{9,10},{10,1... | collective-permute-start | bytes 61448 | tf_op jit(solution)/shard_map/ppermute | solution.py:261
  15.9 20.0 %copy-start = (f32[4]{0:T(128)S(1)}, f32[4]{0:T(128)}, u32[]{:S(2)}) copy-start(f32[4]{0:T(128)} %constant.65) | copy-start | bytes 52
  20.3 15.7 %collective-permute-start.4 = (f32[23,4,640]{2,1,0:T(4,128)S(1)}, f32[23,4,640]{2,1,0:T(4,128)S(1)}, u32[]{:S(2)}, u32[]{:S(2)}) collective-permute-start(f32[23,4,640]{2,1,0:T(4,128)S(1)} %add_add_fusion.1), channel_id=1, source_target_pairs={{0,128},{32,160},{64,192},{96,224},{128,0},{160,32},{192,64},{224,... | collective-permute-start | bytes 706568 | tf_op jit(solution)/shard_map/ppermute | solution.py:251
  36.3 10.2 %collective-permute-start.10 = (f32[23,4,640]{2,1,0:T(4,128)S(1)}, f32[23,4,640]{2,1,0:T(4,128)S(1)}, u32[]{:S(2)}, u32[]{:S(2)}) collective-permute-start(f32[23,4,640]{2,1,0:T(4,128)S(1)} %fusion.13.refs_0_), channel_id=1, source_target_pairs={{0,64},{32,96},{64,0},{96,32},{128,192},{160,224},{192,128},{224,1... | collective-permute-start | bytes 706568 | tf_op jit(solution)/shard_map/ppermute | solution.py:247
  36.5 11.7 %collective-permute-start.7 = (f32[23,4,640]{2,1,0:T(4,128)S(1)}, f32[23,4,640]{2,1,0:T(4,128)S(1)}, u32[]{:S(2)}, u32[]{:S(2)}) collective-permute-start(f32[23,4,640]{2,1,0:T(4,128)S(1)} %fusion.13.refs_0_), channel_id=1, source_target_pairs={{0,32},{32,0},{64,96},{96,64},{128,160},{160,128},{192,224},{224,1... | collective-permute-start | bytes 706568 | tf_op jit(solution)/shard_map/ppermute | solution.py:247
  38.0 13.2 %collective-permute-start.5 = (f32[23,4,640]{2,1,0:T(4,128)S(1)}, f32[23,4,640]{2,1,0:T(4,128)S(1)}, u32[]{:S(2)}, u32[]{:S(2)}) collective-permute-start(f32[23,4,640]{2,1,0:T(4,128)S(1)} %fusion.13.refs_0_), channel_id=1, source_target_pairs={{0,96},{32,64},{64,32},{96,0},{128,224},{160,192},{192,160},{224,1... | collective-permute-start | bytes 706568 | tf_op jit(solution)/shard_map/ppermute | solution.py:247
  48.0 9.5 %collective-permute-start.11 = (f32[23,4,640]{2,1,0:T(4,128)S(1)}, f32[23,4,640]{2,1,0:T(4,128)S(1)}, u32[]{:S(2)}, u32[]{:S(2)}) collective-permute-start(f32[23,4,640]{2,1,0:T(4,128)S(1)} %shard_map.62), channel_id=1, source_target_pairs={{0,64},{32,96},{64,0},{96,32},{128,192},{160,224},{192,128},{224,1... | collective-permute-start | bytes 706568 | tf_op jit(solution)/shard_map/ppermute | solution.py:247
  49.7 7.8 %collective-permute-start.8 = (f32[23,4,640]{2,1,0:T(4,128)S(1)}, f32[23,4,640]{2,1,0:T(4,128)S(1)}, u32[]{:S(2)}, u32[]{:S(2)}) collective-permute-start(f32[23,4,640]{2,1,0:T(4,128)S(1)} %shard_map.60), channel_id=1, source_target_pairs={{0,32},{32,0},{64,96},{96,64},{128,160},{160,128},{192,224},{224,1... | collective-permute-start | bytes 706568 | tf_op jit(solution)/shard_map/ppermute | solution.py:247
  52.7 9.4 %collective-permute-start.9 = (f32[23,4,640]{2,1,0:T(4,128)S(1)}, f32[23,4,640]{2,1,0:T(4,128)S(1)}, u32[]{:S(2)}, u32[]{:S(2)}) collective-permute-start(f32[23,4,640]{2,1,0:T(4,128)S(1)} %shard_map.61), channel_id=1, source_target_pairs={{0,96},{32,64},{64,32},{96,0},{128,224},{160,192},{192,160},{224,1... | collective-permute-start | bytes 706568 | tf_op jit(solution)/shard_map/ppermute | solution.py:247
  56.9 10.6 %collective-permute-start.6 = (f32[2,4,640]{2,1,0:T(4,128)S(1)}, f32[2,4,640]{2,1,0:T(4,128)S(1)}, u32[]{:S(2)}, u32[]{:S(2)}) collective-permute-start(f32[2,4,640]{2,1,0:T(4,128)S(1)} %slice_select_fusion.2), channel_id=1, source_target_pairs={{0,1},{1,2},{2,3},{3,4},{4,5},{5,6},{6,7},{7,8},{8,9},{9,10},{10,1... | collective-permute-start | bytes 61448 | tf_op jit(solution)/shard_map/ppermute | solution.py:261
  62.3 13.1 %collective-permute-start.12 = (f32[23,4,640]{2,1,0:T(4,128)S(1)}, f32[23,4,640]{2,1,0:T(4,128)S(1)}, u32[]{:S(2)}, u32[]{:S(2)}) collective-permute-start(f32[23,4,640]{2,1,0:T(4,128)S(1)} %add_add_fusion), channel_id=1, source_target_pairs={{0,128},{32,160},{64,192},{96,224},{128,0},{160,32},{192,64},{224,... | collective-permute-start | bytes 706568 | tf_op jit(solution)/shard_map/ppermute | solution.py:251
  75.6 13.9 %collective-permute-start.15 = (f32[23,4,640]{2,1,0:T(4,128)S(1)}, f32[23,4,640]{2,1,0:T(4,128)S(1)}, u32[]{:S(2)}, u32[]{:S(2)}) collective-permute-start(f32[23,4,640]{2,1,0:T(4,128)S(1)} %fusion.8.refs_0_), channel_id=1, source_target_pairs={{0,96},{32,64},{64,32},{96,0},{128,224},{160,192},{192,160},{224,1... | collective-permute-start | bytes 706568 | tf_op jit(solution)/shard_map/ppermute | solution.py:247
  76.1 13.4 %collective-permute-start.14 = (f32[23,4,640]{2,1,0:T(4,128)S(1)}, f32[23,4,640]{2,1,0:T(4,128)S(1)}, u32[]{:S(2)}, u32[]{:S(2)}) collective-permute-start(f32[23,4,640]{2,1,0:T(4,128)S(1)} %fusion.8.refs_0_), channel_id=1, source_target_pairs={{0,64},{32,96},{64,0},{96,32},{128,192},{160,224},{192,128},{224,1... | collective-permute-start | bytes 706568 | tf_op jit(solution)/shard_map/ppermute | solution.py:247
  78.2 11.9 %collective-permute-start.13 = (f32[23,4,640]{2,1,0:T(4,128)S(1)}, f32[23,4,640]{2,1,0:T(4,128)S(1)}, u32[]{:S(2)}, u32[]{:S(2)}) collective-permute-start(f32[23,4,640]{2,1,0:T(4,128)S(1)} %fusion.8.refs_0_), channel_id=1, source_target_pairs={{0,32},{32,0},{64,96},{96,64},{128,160},{160,128},{192,224},{224,1... | collective-permute-start | bytes 706568 | tf_op jit(solution)/shard_map/ppermute | solution.py:247
